TPU v7x, 128 devices: a whole 4x4x4 slice. The times are simulated.
128 devices in a mesh: dp: 8 (over y, z_hi), proto: 16 (over z_lo, x, core).
Axes of the slice: x: 4, y: 4, z: 4 (z_hi: 2, z_lo: 2; z = z_hi * 2 + z_lo), core: 2. Of those that a mesh axis runs over, the one named last changes fastest.
Arguments:
- student_patch: bfloat16 [8, 2048, 256], P('dp', 'proto'), may hold values from -4 to 4
- teacher_patch: bfloat16 [8, 2048, 256], P('dp', 'proto'), may hold values from -4 to 4
- patch_image: int32 [8, 2048], P('dp', 'proto'), may hold values from 0 to 7, never falling along the last dimension, each value on 1 to 512 neighbouring positions
- masked_rows: int32 [8, 1024], P('dp', 'proto'), may hold values from 0 to 127, as said below
- student_proto: float32 [256, 131072], P(None, 'proto'), as said below
- teacher_proto: float32 [256, 131072], P(None, 'proto'), as said below
- first_moment: float32 [256, 131072], P('dp', 'proto'), as said below
- second_moment: float32 [256, 131072], P('dp', 'proto'), as said below
- centre: float32 [131072], P('proto'), may hold values from -0.3 to 0.3
Outputs:
- row_grad: float32 [8, 1024, 256], P('dp', 'proto')
- new_student: float32 [256, 131072], P('dp', 'proto')
- new_first: float32 [256, 131072], P('dp', 'proto')
- new_second: float32 [256, 131072], P('dp', 'proto')
- new_teacher: float32 [256, 131072], P('dp', 'proto')
- loss: float32 [], replicated
Inputs may be any that keep to these rules, and one draw needn't show every extreme that they name: `masked_rows`: for each data group and each index of proto in order, 64 distinct positions among that device's 128 patches, ascending; position 0 and position 127 of every device are always masked. `student_proto`: finite entries. `teacher_proto`: finite entries. `first_moment`: finite entries. `second_moment`: positive entries.
All inputs are finite; a program needn't handle non-finite values.
Results may differ from a plain program's by a relative error of at most 0.014.
Values may be sent and summed in bfloat16 or wider, within the bound.
A program may use at most 256 MiB of HBM per device.

v0:
```python
import jax
import jax.numpy as jnp
from jax import lax
from jax.sharding import PartitionSpec as P

PATCH_IMG = 256


student_temp = 0.1
teacher_temp = 0.07
beta_one = 0.9
beta_two = 0.999
fix_one = 0.9999734386011124
fix_two = 0.09520785288629038
learn_rate = 0.002
decay_rate = 0.04
teacher_keep = 0.994


def unit_rows(raw_rows):
    inverse = lax.rsqrt(jnp.sum(raw_rows * raw_rows, axis=-1, keepdims=True) + 1e-06)
    return (raw_rows * inverse, inverse)


def local(
    student_patch,
    teacher_patch,
    patch_image,
    masked_rows,
    student_proto,
    teacher_proto,
    first_moment,
    second_moment,
    centre,
):
    picked = masked_rows[0]
    mask_count = picked.shape[0]
    patch_count = patch_image.shape[1]
    proto_count = lax.axis_size("proto")
    data_count = lax.axis_size("dp")
    raw_student = student_patch[0][picked].astype(jnp.float32)
    raw_teacher = teacher_patch[0][picked].astype(jnp.float32)
    unit_student, inv_student = unit_rows(raw_student)
    unit_teacher, inv_teacher = unit_rows(raw_teacher)
    stacked = jnp.stack([unit_student, unit_teacher]).astype(jnp.bfloat16)
    gathered, image_ids = (
        lax.all_gather(stacked, "proto", axis=1, tiled=True),
        lax.all_gather(patch_image[0][picked], "proto", axis=0, tiled=True),
    )
    rows_student = gathered[0]
    rows_teacher = gathered[1]
    student_w = student_proto.astype(jnp.bfloat16)
    teacher_w = teacher_proto.astype(jnp.bfloat16)
    student_logit = (
        jnp.dot(rows_student, student_w, preferred_element_type=jnp.float32) / student_temp
    )
    teacher_raw = jnp.dot(rows_teacher, teacher_w, preferred_element_type=jnp.float32)
    teacher_logit = (teacher_raw - centre) / teacher_temp
    peak_s, peak_t = lax.pmax(
        (jnp.max(student_logit, axis=1), jnp.max(teacher_logit, axis=1)), "proto"
    )
    exp_s = jnp.exp(student_logit - peak_s[:, None])
    exp_t = jnp.exp(teacher_logit - peak_t[:, None])
    total_s, total_t = lax.psum((jnp.sum(exp_s, axis=1), jnp.sum(exp_t, axis=1)), "proto")
    prob_s = exp_s / total_s[:, None]
    prob_t = exp_t / total_t[:, None]
    labels = jnp.arange(patch_count * proto_count // PATCH_IMG, dtype=jnp.int32)
    matches = (image_ids[:, None] == labels[None, :]).astype(jnp.float32)
    counts = jnp.sum(matches, axis=0)
    per_row = jnp.dot(matches, counts, precision=lax.Precision.HIGHEST)
    row_ratio = mask_count * PATCH_IMG / patch_count
    weights = row_ratio / per_row
    log_total = peak_s + jnp.log(total_s)
    partial_loss = jnp.sum(weights * jnp.sum(prob_t * (log_total[:, None] - student_logit), axis=1))
    grad_logit = (weights[:, None] * (prob_s - prob_t) / student_temp).astype(jnp.bfloat16)
    unit_grad = lax.psum_scatter(
        lax.dot_general(
            grad_logit, student_w, (((1,), (1,)), ((), ())), preferred_element_type=jnp.float32
        ).astype(jnp.bfloat16),
        "proto",
        scatter_dimension=0,
        tiled=True,
    ).astype(jnp.float32)
    row_grad = (
        inv_student * unit_grad
        - inv_student
        * inv_student
        * inv_student
        * raw_student
        * jnp.sum(raw_student * unit_grad, axis=-1, keepdims=True)
    )
    slab_rows = first_moment.shape[0]
    slab_start = lax.axis_index("dp") * slab_rows
    proto_grad = lax.psum_scatter(
        lax.dot_general(
            rows_student, grad_logit, (((0,), (0,)), ((), ())), preferred_element_type=jnp.float32
        ).astype(jnp.bfloat16),
        "dp",
        scatter_dimension=0,
        tiled=True,
    ).astype(jnp.float32)
    loss_sum = lax.psum(partial_loss, ("dp", "proto"))
    rows_total = mask_count * proto_count * data_count
    own_student = lax.dynamic_slice_in_dim(student_proto, slab_start, slab_rows, 0)
    own_teacher = lax.dynamic_slice_in_dim(teacher_proto, slab_start, slab_rows, 0)
    new_first = beta_one * first_moment + (1.0 - beta_one) * proto_grad
    new_second = beta_two * second_moment + (1.0 - beta_two) * proto_grad * proto_grad
    step_size = new_first / fix_one / (jnp.sqrt(new_second / fix_two) + 1e-08)
    new_student = own_student - learn_rate * (step_size + decay_rate * own_student)
    new_teacher = teacher_keep * own_teacher + (1.0 - teacher_keep) * new_student
    loss = loss_sum / rows_total
    return (row_grad[None], new_student, new_first, new_second, new_teacher, loss)


def solution(mesh):
    in_specs = (
        P("dp", "proto", None),
        P("dp", "proto", None),
        P("dp", "proto"),
        P("dp", "proto"),
        P(None, "proto"),
        P(None, "proto"),
        P("dp", "proto"),
        P("dp", "proto"),
        P("proto"),
    )
    out_specs = (
        P("dp", "proto", None),
        P("dp", "proto"),
        P("dp", "proto"),
        P("dp", "proto"),
        P("dp", "proto"),
        P(),
    )
    return jax.shard_map(local, mesh=mesh, in_specs=in_specs, out_specs=out_specs, check_vma=False)
```

profile of v0, /device:TPU:0, one launch (start us, length us, event | category | flops | bytes accessed | tf_op | source)
XLA Modules:
  0.0 365.1 jit_solution(13910082086111725495)
XLA Ops:
  7.2 0.0 copy-start
  7.2 0.0 copy-start.6
  7.2 0.0 all-gather.3.cloned.1.call-start
  7.2 0.7 fusion.27
  7.9 0.1 copy-done
  8.0 0.7 gather_fusion
  8.7 0.1 fusion.20
  8.8 1.5 gather_fusion.2
  10.3 0.1 fusion.19
  10.5 0.1 fusion.18
  10.6 0.6 pad_maximum_fusion
  11.2 0.0 all-gather.3.cloned.1.call-update
  11.2 0.0 reduce-scatter.3.cloned.1.call-start
  11.3 1.4 gather_fusion.1
  12.7 1.2 dynamic-slice
  14.6 0.2 dynamic-update-slice
  14.9 12.9 %all-reduce = s32[1024]{0:T(1024)S(1)} all-reduce(s32[1024]{0:T(1024)S(1)} %dynamic-update-slice), channel_id=2, replica_groups=mesh['dp'=8,'proto'=16] {'proto'}, use_global_device_ids=true, to_apply=%add | all-reduce | flops 1024 | bytes 8192
  27.8 0.1 convert_reduce_fusion
  27.9 0.1 fusion.25
  28.0 18.0 %all-gather.3.cloned.1.call-done = bf16[2,1024,256]{2,1,0:T(8,128)(2,1)} async-done(((bf16[2,64,256]{2,1,0:T(8,128)(2,1)}), bf16[2,1024,256]{2,1,0:T(8,128)(2,1)}) %all-gather.3.cloned.1.call-update) | async-done | bytes 1048592 | tf_op jit(solution)/shard_map/all_gather | solution.py:47
  46.1 0.0 copy-start.3
  46.1 0.0 copy-start.4
  46.1 16.0 %multiply_reduce_fusion.1 = (f32[1024]{0:T(1024)S(1)}, f32[1024,8192]{1,0:T(8,128)}) fusion(f32[256,8192]{1,0:T(8,128)} %param.13, bf16[2,1024,256]{2,1,0:T(8,128)(2,1)} %all-gather.3.cloned.1.call-done), kind=kOutput, calls=%fused_computation.10 | convolution fusion | flops 4313840640 | bytes 42471424 | tf_op jit(solution)/shard_map/dot_general | solution.py:55
  62.0 0.0 copy-done.6
  62.0 0.0 copy-done.3
  62.0 0.0 copy-done.4
  62.0 13.4 %fusion.1 = (f32[1024]{0:T(1024)S(1)}, f32[1024,8192]{1,0:T(8,128)}) fusion(f32[8192]{0:T(1024)S(1)} %copy-done.6, f32[256,8192]{1,0:T(8,128)S(1)} %copy-done.3, bf16[2,1024,256]{2,1,0:T(8,128)(2,1)S(1)} %copy-done.4), kind=kOutput, calls=%fused_computation.9 | convolution fusion | flops 4322229248 | bytes 42504192 | tf_op jit(solution)/shard_map/dot_general | solution.py:57
  75.5 29.6 %all-reduce.2 = (f32[1024]{0:T(1024)S(1)}, f32[1024]{0:T(1024)S(1)}) all-reduce(f32[1024]{0:T(1024)S(1)} %get-tuple-element.18, f32[1024]{0:T(1024)S(1)} %get-tuple-element.20), channel_id=1, replica_groups=mesh['dp'=8,'proto'=16] {'proto'}, use_global_device_ids=true, to_apply=%region_4.0 | all-reduce | flops 2048 | bytes 16384 | tf_op jit(solution)/shard_map/pmax | solution.py:59
  105.0 0.0 copy-start.2
  105.1 15.3 %fusion.3 = f32[1024]{0:T(1024)S(1)} fusion(f32[1024,8192]{1,0:T(8,128)} %get-tuple-element.21, f32[1024]{0:T(1024)S(1)} %get-tuple-element.9, f32[8192]{0:T(1024)S(1)} %copy-done.6), kind=kLoop, calls=%fused_computation.12 | loop fusion | flops 33553408 | bytes 33595392 | tf_op jit(solution)/shard_map/reduce_sum | solution.py:64
  120.4 4.8 %copy-done.2 = f32[1024,8192]{1,0:T(8,128)S(1)} copy-done((f32[1024,8192]{1,0:T(8,128)S(1)}, f32[1024,8192]{1,0:T(8,128)}, u32[]{:S(2)}) %copy-start.2) | copy-done | bytes 33554456
  125.2 6.7 %fusion = f32[1024]{0:T(1024)S(1)} fusion(f32[1024,8192]{1,0:T(8,128)S(1)} %copy-done.2, f32[1024]{0:T(1024)S(1)} %get-tuple-element.8), kind=kLoop, calls=%fused_computation.8 | loop fusion | flops 25164800 | bytes 33562624 | tf_op jit(solution)/shard_map/reduce_sum | solution.py:64
  131.9 27.8 %all-reduce.1 = (f32[1024]{0:T(1024)S(1)}, f32[1024]{0:T(1024)S(1)}) all-reduce(f32[1024]{0:T(1024)S(1)} %fusion, f32[1024]{0:T(1024)S(1)} %fusion.3), channel_id=1, replica_groups=mesh['dp'=8,'proto'=16] {'proto'}, use_global_device_ids=true, to_apply=%region_6.0 | all-reduce | flops 2048 | bytes 16384 | tf_op jit(solution)/shard_map/psum | solution.py:64
  159.7 0.0 copy-start.1
  159.7 31.3 %multiply_reduce_fusion = (f32[1024]{0:T(1024)S(1)}, bf16[1024,8192]{1,0:T(8,128)(2,1)}) fusion(f32[1024,8192]{1,0:T(8,128)} %get-tuple-element.19, f32[1024]{0:T(1024)S(1)} %log_add_fusion, f32[1024]{0:T(1024)S(1)} %get-tuple-element.7, f32[1024]{0:T(1024)S(1)} %get-tuple-element.9, f32[1024,8192]{1,0:T(8,128)} %get-tuple-element.21, f32[8192]{0:T(1024)S(1)} %copy-done.6, ...), kind=kLoop, calls=%fused_computation.3 | loop fusion | flops 117439488 | bytes 83947520 | tf_op jit(solution)/shard_map/reduce_sum | solution.py:74
  191.0 0.0 copy-start.5
  191.0 13.6 %fusion.10 = bf16[1024,256]{1,0:T(8,128)(2,1)} fusion(bf16[1024,8192]{1,0:T(8,128)(2,1)} %get-tuple-element.15, f32[256,8192]{1,0:T(8,128)} %param.13), kind=kOutput, calls=%fused_computation.22 | convolution fusion | flops 4297326592 | bytes 25690112 | tf_op jit(solution)/shard_map/dot_general | solution.py:77
  204.6 0.0 reduce-scatter.3.cloned.1.call-update
  204.6 0.0 reduce-scatter.5.cloned.1.call-start
  204.7 12.1 %convolution_convert_fusion = bf16[256,8192]{1,0:T(8,128)(2,1)} fusion(bf16[1024,8192]{1,0:T(8,128)(2,1)} %get-tuple-element.15, bf16[2,1024,256]{2,1,0:T(8,128)(2,1)S(1)} %copy-done.4), kind=kOutput, calls=%fused_computation.13 | convolution fusion | flops 4297064448 | bytes 21495808 | tf_op jit(solution)/shard_map/dot_general | solution.py:95
  216.7 0.0 reduce-scatter.5.cloned.1.call-update
  216.7 0.6 multiply_reduce_fusion.2
  217.4 66.3 %psum.23 = f32[]{:T(128)} all-reduce(f32[]{:T(128)} %multiply_reduce_fusion.2), channel_id=1, replica_groups=mesh['dp'=8,'proto'=16] {'dp','proto'}, use_global_device_ids=true, to_apply=%region_16.0 | all-reduce | flops 1 | bytes 8 | tf_op jit(solution)/shard_map/psum | solution.py:102
  284.3 0.0 reduce-scatter.3.cloned.1.call-done
  284.3 0.9 fusion.22
  285.2 1.5 fusion.16
  286.7 66.1 %reduce-scatter.5.cloned.1.call-done = bf16[32,8192]{1,0:T(8,128)(2,1)} async-done(((bf16[256,8192]{1,0:T(8,128)(2,1)}), bf16[32,8192]{1,0:T(8,128)(2,1)}) %reduce-scatter.5.cloned.1.call-update) | async-done | bytes 524304 | tf_op jit(solution)/shard_map/reduce_scatter | solution.py:94
  352.7 0.0 copy-done.5
  352.7 4.7 %multiply_add_fusion = (f32[32,8192]{1,0:T(8,128)}, f32[32,8192]{1,0:T(8,128)}, f32[32,8192]{1,0:T(8,128)}, f32[32,8192]{1,0:T(8,128)}) fusion(f32[256,8192]{1,0:T(8,128)} %param.14, s32[]{:T(128)S(6)} %select_n.17, f32[256,8192]{1,0:T(8,128)} %param.13, bf16[32,8192]{1,0:T(8,128)(2,1)} %reduce-scatter.5.cloned.1.call-done, f32[32,8192]{1,0:T(8,128)S(1)} %copy-done.5, ...), kind=kLoop, calls=%fused_computation.25 | loop fusion | flops 4980736 | bytes 8912900 | tf_op jit(solution)/shard_map/add | solution.py:110
  357.4 0.0 copy-done.1
  (6 shorter events, 0.0 us)
Async XLA Ops:
  7.2 0.8 copy-start
  7.2 54.9 %copy-start.6 = (f32[8192]{0:T(1024)S(1)}, f32[8192]{0:T(1024)}, u32[]{:S(2)}) copy-start(f32[8192]{0:T(1024)} %param.17) | copy-start | bytes 98308
  7.2 38.9 %all-gather.3.cloned.1.call-start = ((), (), s32[]{:S(2)}) async-start(), calls=%async_computation.2 | async-start | bytes 1114112 | tf_op jit(solution)/shard_map/all_gather | solution.py:47
  11.2 273.0 %reduce-scatter.3.cloned.1.call-start = ((), (), s32[]{:S(2)}) async-start(), calls=%async_computation.3 | async-start | bytes 557056 | tf_op jit(solution)/shard_map/reduce_scatter | solution.py:76
  46.1 16.0 %copy-start.3 = (f32[256,8192]{1,0:T(8,128)S(1)}, f32[256,8192]{1,0:T(8,128)}, u32[]{:S(2)}) copy-start(f32[256,8192]{1,0:T(8,128)} %param.14) | copy-start | bytes 25165828
  46.1 16.0 %copy-start.4 = (bf16[2,1024,256]{2,1,0:T(8,128)(2,1)S(1)}, bf16[2,1024,256]{2,1,0:T(8,128)(2,1)}, u32[]{:S(2)}) copy-start(bf16[2,1024,256]{2,1,0:T(8,128)(2,1)} %all-gather.3.cloned.1.call-done) | copy-start | bytes 3145732
  105.0 20.2 %copy-start.2 = (f32[1024,8192]{1,0:T(8,128)S(1)}, f32[1024,8192]{1,0:T(8,128)}, u32[]{:S(2)}) copy-start(f32[1024,8192]{1,0:T(8,128)} %get-tuple-element.19) | copy-start | bytes 100663296
  159.7 197.7 %copy-start.1 = (bf16[1,128,256]{2,1,0:T(8,128)(2,1)S(1)}, bf16[1,128,256]{2,1,0:T(8,128)(2,1)}, u32[]{:S(2)}) copy-start(bf16[1,128,256]{2,1,0:T(8,128)(2,1)} %param.9) | copy-start | bytes 196612
  191.0 161.7 %copy-start.5 = (f32[32,8192]{1,0:T(8,128)S(1)}, f32[32,8192]{1,0:T(8,128)}, u32[]{:S(2)}) copy-start(f32[32,8192]{1,0:T(8,128)} %param.15) | copy-start | bytes 3145732
  204.6 148.1 %reduce-scatter.5.cloned.1.call-start = ((), (), s32[]{:S(2)}) async-start(), calls=%async_computation.4 | async-start | bytes 4718592 | tf_op jit(solution)/shard_map/reduce_scatter | solution.py:94
Sparse Core Ops, SparseCore 0:
  11.4 34.6 all-gather.2
  204.7 59.9 reduce-scatter.2
  268.7 84.0 reduce-scatter.4
where the time goes:
time: 366 us; the launch traced here: 365 us
  blocking collectives  137 us (37%)
  waiting for transfers between devices  84.2 us (23%)
  other arithmetic  62.7 us (17%)
  matrix products  55.2 us (15%)
  between operations  16.3 us (4%)
  local copies, waits for them, and re-layouts  10.1 us (3%)
    psum x1, blocking collectives, local(): loss_sum = lax.psum(partial_loss, ('dp', 'proto'))  66.3 us
    reduce_scatter x1, waiting for transfers between devices, local(): lax.psum_scatter(lax.dot_general(rows_student, grad_logit, (((0,), (0,)),...  66.1 us
    reduce_sum x1, other arithmetic, local(): jnp.sum(prob_t * (log_total[:, None] - student_logit), axis=1)  31.3 us
    pmax x1, blocking collectives, local(): lax.pmax((jnp.max(student_logit, axis=1), jnp.max(teacher_logit, axis=1))...  29.6 us
    psum x1, blocking collectives, local(): lax.psum((jnp.sum(exp_s, axis=1), jnp.sum(exp_t, axis=1)), 'proto')  27.8 us
    all_gather x1, waiting for transfers between devices, local(): lax.all_gather(stacked, 'proto', axis=1, tiled=True)  18 us
    dot_general x1, matrix products, local(): jnp.dot(rows_student, student_w, preferred_element_type=jnp.float32)  16 us
    reduce_sum x1, other arithmetic, local(): jnp.sum(exp_t, axis=1)  15.3 us
  transfers between devices with their start and end apart: 3, of which 2 were waited for; matrix products, arithmetic and copies ran while one was open for 5% of the time, Pallas kernels for 0%

commit v1 on v0

v1 whole, which is shorter than its diff:
```python
import functools
import math

import jax
import jax.numpy as jnp
from jax import lax
from jax.experimental import pallas as pl
from jax.experimental.pallas import tpu as pltpu
from jax.sharding import PartitionSpec as P

PATCH_IMG = 256
IMG_GROUP = 8

student_temp = 0.1
teacher_temp = 0.07
beta_one = 0.9
beta_two = 0.999
fix_one = 0.9999734386011124
fix_two = 0.09520785288629038
learn_rate = 0.002
decay_rate = 0.04
teacher_keep = 0.994

F32 = jnp.float32
BF16 = jnp.bfloat16
MESH = pl.DeviceIdType.MESH
LOG2E = math.log2(math.e)
LN2 = math.log(2.0)
SCALE_S = LOG2E / student_temp
SCALE_T = LOG2E / teacher_temp
LOWEST = -3.0e38
LANES = 128


def iota(shape, axis):
    return lax.broadcasted_iota(jnp.int32, shape, axis)


def eye(n):
    return iota((n, n), 0) == iota((n, n), 1)


def to_column(row):
    n = row.shape[1]
    return jnp.sum(jnp.where(eye(n), jnp.broadcast_to(row, (n, n)), 0.0), axis=1, keepdims=True)


def to_row(column):
    n = column.shape[0]
    return jnp.sum(jnp.where(eye(n), jnp.broadcast_to(column, (n, n)), 0.0), axis=0, keepdims=True)


def head_kernel(
    n_dp,
    n_proto,
    student_patch,
    teacher_patch,
    patch_image,
    masked_rows,
    student_hbm,
    teacher_hbm,
    centre,
    row_grad_out,
    proto_grad_out,
    loss_out,
    stage,
    ws,
    wt,
    rows,
    rows_across,
    raw_keep,
    inv_keep,
    ids,
    peak_s,
    sum_s,
    peak_t,
    sum_t,
    weight_tile,
    lse_send,
    lse_all,
    unit_acc,
    unit_send,
    unit_recv,
    slab_send,
    slab_recv,
    loss_send,
    loss_recv,
    group_send,
    group_recv,
    stage_sem,
    row_ssem,
    row_rsem,
    id_ssem,
    id_rsem,
    lse_ssem,
    lse_rsem,
    unit_ssem,
    unit_rsem,
    slab_ssem,
    slab_rsem,
    loss_ssem,
    loss_rsem,
    group_ssem,
    group_rsem,
):
    d = lax.axis_index("dp")
    p = lax.axis_index("proto")
    mask_count = masked_rows.shape[1]
    patch_count = patch_image.shape[1]
    emb, cols = ws.shape
    n_rows = rows.shape[0]
    slab = emb // n_dp
    load_cols = stage.shape[2]
    row_chunk = 256
    n_groups = n_rows // LANES

    def proto_peer(i):
        return lax.rem(p + i, n_proto)

    def dp_peer(i):
        return lax.rem(d + i, n_dp)

    def push(src, dst, ssem, rsem, target):
        return pltpu.make_async_remote_copy(
            src_ref=src, dst_ref=dst, send_sem=ssem, recv_sem=rsem, device_id=target, device_id_type=MESH
        )

    barrier = pltpu.get_barrier_semaphore()
    for i in range(1, n_proto):
        pl.semaphore_signal(barrier, inc=1, device_id=(d, proto_peer(i)), device_id_type=MESH)
    for i in range(1, n_dp):
        pl.semaphore_signal(barrier, inc=1, device_id=(dp_peer(i), p), device_id_type=MESH)

    n_load = cols // load_cols
    n_buf = stage.shape[0]

    def load(hbm, j, slot):
        c0 = pl.multiple_of(j * load_cols, load_cols)
        return pltpu.make_async_copy(hbm.at[:, pl.ds(c0, load_cols)], stage.at[slot], stage_sem.at[slot])

    load(student_hbm, 0, 0).start()
    load(teacher_hbm, 0, 1).start()
    load(student_hbm, 1, 2).start()
    load(teacher_hbm, 1, 3).start()

    picked = to_column(masked_rows[...].astype(F32))
    one_hot = iota((mask_count, patch_count), 1).astype(F32) == picked
    one_hot_f = jnp.where(one_hot, 1.0, 0.0)
    one_hot_b = one_hot_f.astype(BF16)
    own = pl.ds(pl.multiple_of(p * mask_count, mask_count), mask_count)
    raw_s = jnp.dot(one_hot_b, student_patch[...], preferred_element_type=F32)
    raw_t = jnp.dot(one_hot_b, teacher_patch[...], preferred_element_type=F32)
    inv_s = lax.rsqrt(jnp.sum(raw_s * raw_s, axis=1, keepdims=True) + 1e-06)
    inv_t = lax.rsqrt(jnp.sum(raw_t * raw_t, axis=1, keepdims=True) + 1e-06)
    rows[own, :emb] = (raw_s * inv_s).astype(BF16)
    rows[own, emb:] = (raw_t * inv_t).astype(BF16)
    raw_keep[...] = raw_s
    inv_keep[...] = jnp.broadcast_to(inv_s, inv_keep.shape)
    own_ids = to_row(jnp.sum(one_hot_f * patch_image[...].astype(F32), axis=1, keepdims=True))
    ids[p] = jnp.broadcast_to(jnp.concatenate([own_ids, own_ids], axis=1), (8, LANES))

    pl.semaphore_wait(barrier, n_proto + n_dp - 2)

    def block_of(q):
        return rows.at[pl.ds(pl.multiple_of(q * mask_count, mask_count), mask_count)]

    twin = p + 1 - 2 * lax.rem(p, 2)
    sends = []
    for i in range(2, n_proto, 2):
        sends.append(push(block_of(p), block_of(p), row_ssem.at[i], row_rsem.at[p], (d, proto_peer(i))))
    sends.append(push(block_of(p), block_of(p), row_ssem.at[0], row_rsem.at[p], (d, twin)))
    for i in range(1, n_proto):
        sends.append(push(ids.at[p], ids.at[p], id_ssem.at[i], id_rsem.at[p], (d, proto_peer(i))))
    for copy in sends:
        copy.start()

    def cast_step(j, carry):
        c0 = pl.multiple_of(j * load_cols, load_cols)
        odd = lax.rem(j, 2) * 2
        load(student_hbm, j, odd).wait()
        ws[:, pl.ds(c0, load_cols)] = stage[odd].astype(BF16)

        @pl.when(j + 2 < n_load)
        def _():
            load(student_hbm, j + 2, odd).start()

        load(teacher_hbm, j, odd + 1).wait()
        wt[:, pl.ds(c0, load_cols)] = stage[odd + 1].astype(BF16)

        @pl.when(j + 2 < n_load)
        def _():
            load(teacher_hbm, j + 2, odd + 1).start()

        return carry

    lax.fori_loop(0, n_load, cast_step, 0)

    forwards = []
    for i in range(2, n_proto, 2):
        q = lax.rem(p + n_proto - i, n_proto)
        push(block_of(q), block_of(q), row_ssem.at[i], row_rsem.at[q], (d, twin)).wait_recv()
        forward = push(block_of(q), block_of(q), row_ssem.at[i + 1], row_rsem.at[q], (d, twin))
        forward.start()
        forwards.append(forward)
    push(block_of(twin), block_of(twin), row_ssem.at[0], row_rsem.at[twin], (d, twin)).wait_recv()
    for i in range(2, n_proto, 2):
        q = lax.rem(twin + n_proto - i, n_proto)
        push(block_of(q), block_of(q), row_ssem.at[i], row_rsem.at[q], (d, twin)).wait_recv()
    for i in range(1, n_proto):
        q = lax.rem(p + n_proto - i, n_proto)
        push(ids.at[q], ids.at[q], id_ssem.at[i], id_rsem.at[q], (d, twin)).wait_recv()

    lane = iota((1, LANES), 1)
    id_rows = [
        jnp.where(lane < mask_count, ids[2 * g, 0:1, :], ids[2 * g + 1, 0:1, :]) for g in range(n_groups)
    ]
    id_tile = jnp.concatenate(id_rows, axis=0)
    weight = jnp.zeros_like(id_tile)
    row_ratio = float(mask_count * PATCH_IMG // patch_count)
    for label in range(IMG_GROUP):
        match = id_tile == float(label)
        hits = jnp.where(match, 1.0, 0.0)
        count = jnp.sum(jnp.sum(hits, axis=0, keepdims=True), axis=1, keepdims=True)
        weight = weight + hits * (row_ratio / jnp.maximum(count, 1.0))
    weight_tile[...] = weight

    for peak, total in ((peak_s, sum_s), (peak_t, sum_t)):
        peak[...] = jnp.full(peak.shape, LOWEST, F32)
        total[...] = jnp.zeros(total.shape, F32)
    cols_one = 512

    def first_step(j, carry):
        c0 = pl.multiple_of(j * cols_one, cols_one)
        for r in range(n_rows // row_chunk):
            part = slice(r * row_chunk, (r + 1) * row_chunk)
            for e0, w, peak, total, scale, shift in (
                (0, ws, peak_s, sum_s, SCALE_S, False),
                (emb, wt, peak_t, sum_t, SCALE_T, True),
            ):
                z = jnp.dot(rows[part, e0 : e0 + emb], w[:, pl.ds(c0, cols_one)], preferred_element_type=F32)
                if shift:
                    z = z - centre[:, pl.ds(c0, cols_one)]
                pieces = [z[:, k * LANES : (k + 1) * LANES] for k in range(cols_one // LANES)]
                before = peak[part, :]
                now = before
                for piece in pieces:
                    now = jnp.maximum(now, piece)
                acc = total[part, :] * jnp.exp2((before - now) * scale)
                for piece in pieces:
                    acc = acc + jnp.exp2((piece - now) * scale)
                total[part, :] = acc
                peak[part, :] = now
        return carry

    lax.fori_loop(0, cols // cols_one, first_step, 0)

    for k, (peak, total, scale) in enumerate(((peak_s, sum_s, SCALE_S), (peak_t, sum_t, SCALE_T))):
        for g in range(n_groups):
            part = slice(g * LANES, (g + 1) * LANES)
            lanes_peak = peak[part, :]
            top = jnp.max(lanes_peak, axis=1, keepdims=True)
            mass = jnp.sum(total[part, :] * jnp.exp2((lanes_peak - top) * scale), axis=1, keepdims=True)
            r = k * n_groups + g
            lse_send[r : r + 1, :] = to_row(top * scale + jnp.log(mass) * LOG2E)
    lse_all[p] = lse_send[...]
    lse_copies = []
    for i in range(1, n_proto):
        lse_copies.append(
            push(lse_send, lse_all.at[p], lse_ssem.at[i], lse_rsem.at[p], (d, proto_peer(i)))
        )
    for copy in lse_copies:
        copy.start()

    rows_across[...] = rows[:, :emb].T
    unit_acc[...] = jnp.zeros(unit_acc.shape, F32)

    for i in range(1, n_proto):
        q = lax.rem(p + n_proto - i, n_proto)
        push(lse_send, lse_all.at[q], lse_ssem.at[i], lse_rsem.at[q], (d, twin)).wait_recv()
    top = lse_all[0]
    for q in range(1, n_proto):
        top = jnp.maximum(top, lse_all[q])
    mass = jnp.exp2(lse_all[0] - top)
    for q in range(1, n_proto):
        mass = mass + jnp.exp2(lse_all[q] - top)
    lse = top + jnp.log(mass) * LOG2E
    lse_rows_s = lse[:n_groups]
    gain = jnp.log(weight_tile[...] / student_temp) * LOG2E
    shift_s = lse_rows_s - gain
    shift_t = lse[n_groups:] - gain
    for g in range(n_groups):
        part = slice(g * LANES, (g + 1) * LANES)
        peak_s[part, :] = jnp.broadcast_to(to_column(shift_s[g : g + 1, :]), (LANES, LANES))
        peak_t[part, :] = jnp.broadcast_to(to_column(shift_t[g : g + 1, :]), (LANES, LANES))

    cols_two = 1024
    loss_send[...] = jnp.zeros(loss_send.shape, F32)

    def second_step(j, carry):
        c0 = pl.multiple_of(j * cols_two, cols_two)
        block = pl.ds(c0, cols_two)
        w_block = ws[:, block]
        wt_block = wt[:, block]
        shift = centre[:, block] * SCALE_T
        acc = jnp.zeros((emb, cols_two), F32)
        cross = jnp.zeros((row_chunk, LANES), F32)
        for r in range(n_rows // row_chunk):
            part = slice(r * row_chunk, (r + 1) * row_chunk)
            zs = jnp.dot(rows[part, :emb], w_block, preferred_element_type=F32)
            zt = jnp.dot(rows[part, emb:], wt_block, preferred_element_type=F32)
            a = peak_s[part, :]
            b = peak_t[part, :]
            pieces = []
            for k in range(cols_two // LANES):
                at = slice(k * LANES, (k + 1) * LANES)
                z = zs[:, at]
                target = jnp.exp2(zt[:, at] * SCALE_T - (b + shift[:, at]))
                pieces.append((jnp.exp2(z * SCALE_S - a) - target).astype(BF16))
                cross = cross + target * z
            glog = jnp.concatenate(pieces, axis=1)
            unit_acc[part, :] += lax.dot_general(
                glog, w_block, (((1,), (1,)), ((), ())), preferred_element_type=F32
            )
            acc = acc + jnp.dot(rows_across[:, part], glog, preferred_element_type=F32)
        slab_send[:, :, block] = acc.astype(BF16).reshape(n_dp, slab, cols_two)
        loss_send[...] += jnp.sum(cross.reshape(row_chunk // 8, 8, LANES), axis=0)
        for i in range(1, n_dp):
            t = dp_peer(i)
            push(
                slab_send.at[t, :, block], slab_recv.at[d, :, block], slab_ssem.at[i], slab_rsem.at[d], (t, p)
            ).start()
        return carry

    lax.fori_loop(0, cols // cols_two, second_step, 0)

    unit_send[...] = unit_acc[...].astype(BF16)
    loss_recv[p] = loss_send[...]
    tails = []
    for i in range(1, n_proto):
        q = proto_peer(i)
        tails.append(push(loss_send, loss_recv.at[p], loss_ssem.at[i], loss_rsem.at[p], (d, q)))
        at = pl.ds(pl.multiple_of(q * mask_count, mask_count), mask_count)
        tails.append(push(unit_send.at[at], unit_recv.at[p], unit_ssem.at[i], unit_rsem.at[p], (d, q)))
    for copy in tails:
        copy.start()
    unit_recv[p] = unit_send[own, :]

    for i in range(1, n_proto):
        q = lax.rem(p + n_proto - i, n_proto)
        push(loss_send, loss_recv.at[q], loss_ssem.at[i], loss_rsem.at[q], (d, twin)).wait_recv()
    cross_total = loss_recv[0]
    for q in range(1, n_proto):
        cross_total = cross_total + loss_recv[q]
    group_send[...] = weight_tile[...] * lse_rows_s * LN2 - cross_total
    group_recv[d] = group_send[...]
    group_copies = []
    for i in range(1, n_dp):
        group_copies.append(
            push(group_send, group_recv.at[d], group_ssem.at[i], group_rsem.at[d], (dp_peer(i), p))
        )
    for copy in group_copies:
        copy.start()

    for i in range(1, n_proto):
        q = lax.rem(p + n_proto - i, n_proto)
        push(unit_send.at[own], unit_recv.at[q], unit_ssem.at[i], unit_rsem.at[q], (d, twin)).wait_recv()
    unit_grad = unit_recv[0].astype(F32)
    for q in range(1, n_proto):
        unit_grad = unit_grad + unit_recv[q].astype(F32)
    raw = raw_keep[...]
    inv = inv_keep[:, 0:1]
    dotted = jnp.sum(raw * unit_grad, axis=1, keepdims=True)
    row_grad_out[...] = inv * unit_grad - (inv * inv * inv) * raw * dotted

    for i in range(1, n_dp):
        q = lax.rem(d + n_dp - i, n_dp)
        push(group_send, group_recv.at[q], group_ssem.at[i], group_rsem.at[q], (d, twin)).wait_recv()
    total = group_recv[0]
    for q in range(1, n_dp):
        total = total + group_recv[q]
    total = jnp.sum(jnp.sum(total, axis=0, keepdims=True), axis=1, keepdims=True)
    loss_out[...] = jnp.broadcast_to(total / float(n_rows * n_dp), loss_out.shape)

    for i in range(1, n_dp):
        q = lax.rem(d + n_dp - i, n_dp)
        push(slab_send.at[d], slab_recv.at[q], slab_ssem.at[i], slab_rsem.at[q], (d, twin)).wait_recv()
    slab_recv[d] = slab_send[d]

    def sum_step(j, carry):
        block = pl.ds(pl.multiple_of(j * 1024, 1024), 1024)
        acc = slab_recv[0, :, block].astype(F32)
        for q in range(1, n_dp):
            acc = acc + slab_recv[q, :, block].astype(F32)
        proto_grad_out[:, block] = acc
        return carry

    lax.fori_loop(0, cols // 1024, sum_step, 0)

    for copy in sends + forwards + lse_copies + tails + group_copies:
        copy.wait_send()
    for i in range(1, n_dp):
        t = dp_peer(i)
        push(slab_send.at[t], slab_recv.at[d], slab_ssem.at[i], slab_rsem.at[d], (t, p)).wait_send()


def head(n_dp, n_proto, student_patch, teacher_patch, patch_image, masked_rows, student_proto, teacher_proto, centre):
    mask_count = masked_rows.shape[1]
    emb, cols = student_proto.shape
    n_rows = mask_count * n_proto
    vmem = pl.BlockSpec(memory_space=pltpu.VMEM)
    hbm = pl.BlockSpec(memory_space=pl.ANY)
    dma = pltpu.SemaphoreType.DMA
    slab = emb // n_dp
    n_groups = n_rows // LANES
    return pl.pallas_call(
        functools.partial(head_kernel, n_dp, n_proto),
        out_shape=(
            jax.ShapeDtypeStruct((mask_count, emb), F32),
            jax.ShapeDtypeStruct((slab, cols), F32),
            jax.ShapeDtypeStruct((8, LANES), F32),
        ),
        in_specs=[vmem, vmem, vmem, vmem, hbm, hbm, vmem],
        out_specs=(vmem, vmem, vmem),
        scratch_shapes=[
            pltpu.VMEM((4, emb, 1024), F32),
            pltpu.VMEM((emb, cols), BF16),
            pltpu.VMEM((emb, cols), BF16),
            pltpu.VMEM((n_rows, 2 * emb), BF16),
            pltpu.VMEM((emb, n_rows), BF16),
            pltpu.VMEM((mask_count, emb), F32),
            pltpu.VMEM((mask_count, LANES), F32),
            pltpu.VMEM((n_proto, 8, LANES), F32),
            pltpu.VMEM((n_rows, LANES), F32),
            pltpu.VMEM((n_rows, LANES), F32),
            pltpu.VMEM((n_rows, LANES), F32),
            pltpu.VMEM((n_rows, LANES), F32),
            pltpu.VMEM((n_groups, LANES), F32),
            pltpu.VMEM((2 * n_groups, LANES), F32),
            pltpu.VMEM((n_proto, 2 * n_groups, LANES), F32),
            pltpu.VMEM((n_rows, emb), F32),
            pltpu.VMEM((n_rows, emb), BF16),
            pltpu.VMEM((n_proto, mask_count, emb), BF16),
            pltpu.VMEM((n_dp, slab, cols), BF16),
            pltpu.VMEM((n_dp, slab, cols), BF16),
            pltpu.VMEM((8, LANES), F32),
            pltpu.VMEM((n_proto, 8, LANES), F32),
            pltpu.VMEM((8, LANES), F32),
            pltpu.VMEM((n_dp, 8, LANES), F32),
            dma((4,)),
        ]
        + [dma((n_proto,))] * 8
        + [dma((n_dp,))] * 2
        + [dma((n_proto,))] * 2
        + [dma((n_dp,))] * 2,
        compiler_params=pltpu.CompilerParams(
            collective_id=0, has_side_effects=True, vmem_limit_bytes=60 * 1024 * 1024
        ),
        name="head",
    )(student_patch, teacher_patch, patch_image, masked_rows, student_proto, teacher_proto, centre)


def local(
    student_patch,
    teacher_patch,
    patch_image,
    masked_rows,
    student_proto,
    teacher_proto,
    first_moment,
    second_moment,
    centre,
):
    n_proto = lax.axis_size("proto")
    n_dp = lax.axis_size("dp")
    row_grad, proto_grad, loss = head(
        n_dp,
        n_proto,
        student_patch[0],
        teacher_patch[0],
        patch_image,
        masked_rows,
        student_proto,
        teacher_proto,
        centre[None, :],
    )
    slab_rows = first_moment.shape[0]
    slab_start = lax.axis_index("dp") * slab_rows
    own_student = lax.dynamic_slice_in_dim(student_proto, slab_start, slab_rows, 0)
    own_teacher = lax.dynamic_slice_in_dim(teacher_proto, slab_start, slab_rows, 0)
    new_first = beta_one * first_moment + (1.0 - beta_one) * proto_grad
    new_second = beta_two * second_moment + (1.0 - beta_two) * proto_grad * proto_grad
    step_size = new_first / fix_one / (jnp.sqrt(new_second / fix_two) + 1e-08)
    new_student = own_student - learn_rate * (step_size + decay_rate * own_student)
    new_teacher = teacher_keep * own_teacher + (1.0 - teacher_keep) * new_student
    return (row_grad[None], new_student, new_first, new_second, new_teacher, loss[0, 0])


def solution(mesh):
    in_specs = (
        P("dp", "proto", None),
        P("dp", "proto", None),
        P("dp", "proto"),
        P("dp", "proto"),
        P(None, "proto"),
        P(None, "proto"),
        P("dp", "proto"),
        P("dp", "proto"),
        P("proto"),
    )
    out_specs = (
        P("dp", "proto", None),
        P("dp", "proto"),
        P("dp", "proto"),
        P("dp", "proto"),
        P("dp", "proto"),
        P(),
    )
    return jax.shard_map(local, mesh=mesh, in_specs=in_specs, out_specs=out_specs, check_vma=False)
```

time: 366 us -> 116 us (0.32)
  blocking collectives: 137 us -> 0 us
  Pallas kernels: 0 us -> 108 us
  waiting for transfers between devices: 84.2 us -> 0 us
  other arithmetic: 62.7 us -> 4.46 us
  matrix products: 55.2 us -> 0 us
  between operations: 16.3 us -> 0.67 us
  local copies, waits for them, and re-layouts: 10.1 us -> 1.86 us
    pallas_call x0 -> x1, Pallas kernels: none -> 108 us  [head(): pl.pallas_call(functools.partial(head_kernel, n_dp, n_proto), out_shape=(...]
    psum x2 -> x0, blocking collectives: 94.1 us -> none  [the longest x1 66.3 us: local(): loss_sum = lax.psum(partial_loss, ('dp', 'proto'))]
    reduce_scatter x2 -> x0, waiting for transfers between devices: 66.1 us -> none  [the longest x1 66.1 us: local(): lax.psum_scatter(lax.dot_general(rows_student, grad_logit, (((0,), (0,)),...]
    dot_general x5 -> x0, matrix products: 55.2 us -> none  [the longest x1 16 us: local(): jnp.dot(rows_student, student_w, preferred_element_type=jnp.float32)]
    reduce_sum x8 -> x0, other arithmetic: 55.1 us -> none  [the longest x1 31.3 us: local(): jnp.sum(prob_t * (log_total[:, None] - student_logit), axis=1)]
    pmax x1 -> x0, blocking collectives: 29.6 us -> none  [local(): lax.pmax((jnp.max(student_logit, axis=1), jnp.max(teacher_logit, axis=1))...]
    all_gather x1 -> x0, waiting for transfers between devices: 18 us -> none  [local(): lax.all_gather(stacked, 'proto', axis=1, tiled=True)]
    unnamed x1 -> x0, blocking collectives: 12.9 us -> none
  transfers between devices with their start and end apart: 3 -> 0, of which waited for: 2 -> 0; matrix products, arithmetic and copies ran while one was open for 5% -> 0% of each run, Pallas kernels for 0% -> 0%
where the time goes in v1:
time: 116 us; the launch traced here: 115 us
  Pallas kernels  108 us (93%)
  other arithmetic  4.46 us (4%)
  local copies, waits for them, and re-layouts  1.86 us (2%)
    pallas_call x1, Pallas kernels, head(): pl.pallas_call(functools.partial(head_kernel, n_dp, n_proto), out_shape=(...  108 us
    add x1, other arithmetic, local(): teacher_keep * own_teacher + (1.0 - teacher_keep) * new_student  4.46 us

profile of v1, /device:TPU:0, one launch (start us, length us, event | category | flops | bytes accessed | tf_op | source)
XLA Modules:
  0.0 115.2 jit_solution(4338601560514582476)
XLA Ops:
  0.6 0.0 copy-start
  0.6 0.0 copy-start.1
  0.7 108.2 %head.1 = (f32[64,256]{1,0:T(8,128)}, f32[32,8192]{1,0:T(8,128)}, f32[8,128]{1,0:T(8,128)}) custom-call(bf16[128,256]{1,0:T(8,128)(2,1)} %bitcast.5, bf16[128,256]{1,0:T(8,128)(2,1)} %bitcast.6, s32[1,128]{1,0:T(1,128)} %patch_image.1, s32[1,64]{1,0:T(1,128)} %masked_rows.1, f32[256,8192]{1,0:T(8,128)} %student_hbm.1, f32[256,8192]{1,0:T(8,128)} %teacher_hbm.1, ...), custom_call_target="tpu_custom_call" | custom-call | tf_op jit(solution)/shard_map/head/pallas_call | solution.py:415
  108.8 0.0 copy-start.2
  108.9 1.2 %slice.3 = f32[1,1]{1,0:T(1,128)} slice(f32[8,128]{1,0:T(8,128)} %get-tuple-element.11), slice={[0:1], [0:1]} | slice | bytes 8 | tf_op jit(solution)/shard_map/slice | solution.py:495
  110.1 0.0 copy-done
  110.1 0.0 copy-done.1
  110.1 4.5 %multiply_add_fusion = (f32[32,8192]{1,0:T(8,128)}, f32[32,8192]{1,0:T(8,128)}, f32[32,8192]{1,0:T(8,128)}, f32[32,8192]{1,0:T(8,128)}) fusion(f32[256,8192]{1,0:T(8,128)} %teacher_hbm.1, s32[]{:T(128)S(6)} %select_n.4, f32[256,8192]{1,0:T(8,128)} %student_hbm.1, f32[32,8192]{1,0:T(8,128)} %get-tuple-element.10, f32[32,8192]{1,0:T(8,128)S(1)} %copy-done, ...), kind=kLoop, calls=%fused_computation.2 | loop fusion | flops 4718592 | bytes 9437188 | tf_op jit(solution)/shard_map/add | solution.py:494
  114.5 0.0 copy-done.2
  114.5 0.6 copy.16
Async XLA Ops:
  0.6 109.4 %copy-start = (f32[32,8192]{1,0:T(8,128)S(1)}, f32[32,8192]{1,0:T(8,128)}, u32[]{:S(2)}) copy-start(f32[32,8192]{1,0:T(8,128)} %param.15) | copy-start | bytes 3145732
  0.6 109.4 %copy-start.1 = (f32[32,8192]{1,0:T(8,128)S(1)}, f32[32,8192]{1,0:T(8,128)}, u32[]{:S(2)}) copy-start(f32[32,8192]{1,0:T(8,128)} %param.16) | copy-start | bytes 3145732
  108.8 5.7 %copy-start.2 = (f32[64,256]{1,0:T(8,128)S(1)}, f32[64,256]{1,0:T(8,128)}, u32[]{:S(2)}) copy-start(f32[64,256]{1,0:T(8,128)} %get-tuple-element.9) | copy-start | bytes 196612

commit v2 on v1

v2 whole, which is shorter than its diff:
```python
import functools
import math

import jax
import jax.numpy as jnp
from jax import lax
from jax.experimental import pallas as pl
from jax.experimental.pallas import tpu as pltpu
from jax.sharding import PartitionSpec as P

PATCH_IMG = 256
IMG_GROUP = 8

student_temp = 0.1
teacher_temp = 0.07
beta_one = 0.9
beta_two = 0.999
fix_one = 0.9999734386011124
fix_two = 0.09520785288629038
learn_rate = 0.002
decay_rate = 0.04
teacher_keep = 0.994

F32 = jnp.float32
BF16 = jnp.bfloat16
MESH = pl.DeviceIdType.MESH
LOG2E = math.log2(math.e)
LN2 = math.log(2.0)
SCALE_S = LOG2E / student_temp
SCALE_T = LOG2E / teacher_temp
LOWEST = -3.0e38
LANES = 128
HALVES = 2


def iota(shape, axis):
    return lax.broadcasted_iota(jnp.int32, shape, axis)


def eye(n):
    return iota((n, n), 0) == iota((n, n), 1)


def to_column(row):
    n = row.shape[1]
    return jnp.sum(jnp.where(eye(n), jnp.broadcast_to(row, (n, n)), 0.0), axis=1, keepdims=True)


def to_row(column):
    n = column.shape[0]
    return jnp.sum(jnp.where(eye(n), jnp.broadcast_to(column, (n, n)), 0.0), axis=0, keepdims=True)


def head_kernel(
    n_dp,
    n_proto,
    student_patch,
    teacher_patch,
    patch_image,
    masked_rows,
    student_hbm,
    teacher_hbm,
    centre,
    row_grad_out,
    proto_grad_out,
    loss_out,
    stage,
    ws,
    wt,
    rows,
    rows_across,
    raw_keep,
    inv_keep,
    ids,
    peak_s,
    sum_s,
    peak_t,
    sum_t,
    shift_s,
    shift_t,
    weight_tile,
    lse_tile,
    lse_send,
    lse_all,
    unit_acc,
    unit_send,
    unit_recv,
    slab_send,
    slab_recv,
    both,
    half_send,
    half_recv,
    loss_acc,
    loss_send,
    loss_recv,
    group_recv,
    stage_sem,
    row_ssem,
    hand_ssem,
    row_rsem,
    id_ssem,
    id_rsem,
    lse_ssem,
    lse_rsem,
    unit_ssem,
    unit_rsem,
    slab_ssem,
    slab_rsem,
    half_ssem,
    half_rsem,
    loss_ssem,
    loss_rsem,
    group_ssem,
    group_rsem,
):
    n_y = n_dp // HALVES
    n_plane = HALVES * n_proto
    n_z = 2 * HALVES
    n_x = n_plane // (2 * n_z)
    d = lax.axis_index("dp")
    p = lax.axis_index("proto")
    y = d // HALVES
    zh = lax.rem(d, HALVES)
    me = zh * n_proto + p
    z = me // (2 * n_x)
    x = lax.rem(me // 2, n_x)
    core = lax.rem(p, 2)
    twin = me + 1 - 2 * core
    mask_count = masked_rows.shape[1]
    patch_count = patch_image.shape[1]
    emb, cols = ws.shape
    n_rows = rows.shape[0]
    chunk = n_rows // n_z
    slab = emb // n_y
    part_rows = slab // HALVES
    load_cols = stage.shape[2]
    row_chunk = 256
    tiles = chunk // LANES
    group_tiles = n_rows // LANES // HALVES
    first_col = zh * cols

    def place(q):
        return (HALVES * y + q // n_proto, lax.rem(q, n_proto))

    def ring(i):
        return lax.rem(me + i, n_plane)

    def back(i):
        return lax.rem(me + n_plane - i, n_plane)

    def push(src, dst, ssem, rsem, target):
        return pltpu.make_async_remote_copy(
            src_ref=src, dst_ref=dst, send_sem=ssem, recv_sem=rsem, device_id=target, device_id_type=MESH
        )

    def each(count, body):
        def step(i, carry):
            body(i)
            return carry

        lax.fori_loop(1, count, step, 0)

    barrier = pltpu.get_barrier_semaphore()

    def y_peer(i):
        return (HALVES * lax.rem(y + i, n_y) + zh, p)

    each(n_plane, lambda i: pl.semaphore_signal(barrier, inc=1, device_id=place(ring(i)), device_id_type=MESH))
    each(n_y, lambda i: pl.semaphore_signal(barrier, inc=1, device_id=y_peer(i), device_id_type=MESH))

    n_load = cols // load_cols

    def load(hbm, j, slot):
        c0 = pl.multiple_of(first_col + j * load_cols, load_cols)
        return pltpu.make_async_copy(hbm.at[:, pl.ds(c0, load_cols)], stage.at[slot], stage_sem.at[slot])

    load(student_hbm, 0, 0).start()
    load(teacher_hbm, 0, 1).start()
    load(student_hbm, 1, 2).start()
    load(teacher_hbm, 1, 3).start()

    picked = to_column(masked_rows[...].astype(F32))
    one_hot = iota((mask_count, patch_count), 1).astype(F32) == picked
    one_hot_f = jnp.where(one_hot, 1.0, 0.0)
    one_hot_b = one_hot_f.astype(BF16)
    raw_s = jnp.dot(one_hot_b, student_patch[...], preferred_element_type=F32)
    raw_t = jnp.dot(one_hot_b, teacher_patch[...], preferred_element_type=F32)
    inv_s = lax.rsqrt(jnp.sum(raw_s * raw_s, axis=1, keepdims=True) + 1e-06)
    inv_t = lax.rsqrt(jnp.sum(raw_t * raw_t, axis=1, keepdims=True) + 1e-06)

    def span(q):
        return pl.ds(pl.multiple_of(q * mask_count, mask_count), mask_count)

    rows[span(me), :emb] = (raw_s * inv_s).astype(BF16)
    rows[span(me), emb:] = (raw_t * inv_t).astype(BF16)
    raw_keep[...] = raw_s
    inv_keep[...] = jnp.broadcast_to(inv_s, inv_keep.shape)
    own_ids = to_row(jnp.sum(one_hot_f * patch_image[...].astype(F32), axis=1, keepdims=True))
    ids[me] = jnp.concatenate([own_ids, own_ids], axis=1)

    pl.semaphore_wait(barrier, n_plane + n_y - 2)

    def at(z_at, x_at):
        return (lax.rem(z_at, n_z) * n_x + lax.rem(x_at, n_x)) * 2 + core

    def row_copy(dz, dx):
        i = dz * n_x + dx
        block = rows.at[span(me)]
        return push(block, block, row_ssem.at[i], row_rsem.at[me], place(at(z + dz, x + dx)))

    def row_arrival(q):
        block = rows.at[span(q)]
        return push(block, block, row_ssem.at[0], row_rsem.at[q], place(twin))

    def hand_on(dz, dx):
        q = at(z + n_z - dz, x + n_x - dx)
        block = rows.at[span(q)]
        return push(block, block, hand_ssem.at[dz * n_x + dx], row_rsem.at[q], place(twin))

    hand_on(0, 0).start()
    order = [0, 1, 3, 2]
    for dz in order:
        for dx in order:
            if dz or dx:
                row_copy(dz, dx).start()

    def id_copy(i):
        return push(ids.at[me], ids.at[me], id_ssem.at[i], id_rsem.at[me], place(ring(i)))

    each(n_plane, lambda i: id_copy(i).start())

    def cast_step(j, carry):
        c0 = pl.multiple_of(j * load_cols, load_cols)
        odd = lax.rem(j, 2) * 2
        load(student_hbm, j, odd).wait()
        ws[:, pl.ds(c0, load_cols)] = stage[odd].astype(BF16)

        @pl.when(j + 2 < n_load)
        def _():
            load(student_hbm, j + 2, odd).start()

        load(teacher_hbm, j, odd + 1).wait()
        wt[:, pl.ds(c0, load_cols)] = stage[odd + 1].astype(BF16)

        @pl.when(j + 2 < n_load)
        def _():
            load(teacher_hbm, j + 2, odd + 1).start()

        return carry

    lax.fori_loop(0, n_load, cast_step, 0)

    def take_direct(dz, skip_own=False):
        for dx in order:
            if not (skip_own and dx == 0):
                row_arrival(at(z + n_z - dz, x + n_x - dx)).wait_recv()
                hand_on(dz, dx).start()

    def take_handed(dz):
        for dx in order:
            row_arrival(at(z + n_z - dz, x + n_x - dx) + 1 - 2 * core).wait_recv()

    take_direct(0, skip_own=True)
    take_handed(0)

    cols_one = 512
    n_one = cols // cols_one

    def lse_copy(k_at, i):
        return push(
            lse_send.at[k_at], lse_all.at[k_at, me], lse_ssem.at[k_at, i], lse_rsem.at[k_at, me], place(ring(i))
        )

    def chunk_step(k, carry):
        dz = k + (k // 2) * (1 - 2 * lax.rem(k, 2))
        after = k + 1
        dz_after = after + (after // 2) * (1 - 2 * lax.rem(after, 2))
        z_at = lax.rem(z + n_z - dz, n_z)
        for peak, total in ((peak_s, sum_s), (peak_t, sum_t)):
            peak[...] = jnp.full(peak.shape, LOWEST, F32)
            total[...] = jnp.zeros(total.shape, F32)

        def first_step(j, inner):
            c0 = pl.multiple_of(j * cols_one, cols_one)
            for r in range(chunk // row_chunk):
                part = slice(r * row_chunk, (r + 1) * row_chunk)
                here = pl.ds(pl.multiple_of(z_at * chunk + r * row_chunk, row_chunk), row_chunk)
                for e0, w, peak, total, scale, shift in (
                    (0, ws, peak_s, sum_s, SCALE_S, False),
                    (emb, wt, peak_t, sum_t, SCALE_T, True),
                ):
                    logit = jnp.dot(
                        rows[here, e0 : e0 + emb], w[:, pl.ds(c0, cols_one)], preferred_element_type=F32
                    )
                    if shift:
                        logit = logit - centre[:, pl.ds(pl.multiple_of(first_col + c0, cols_one), cols_one)]
                    pieces = [logit[:, n * LANES : (n + 1) * LANES] for n in range(cols_one // LANES)]
                    before = peak[part, :]
                    now = before
                    for piece in pieces:
                        now = jnp.maximum(now, piece)
                    acc = total[part, :] * jnp.exp2((before - now) * scale)
                    for piece in pieces:
                        acc = acc + jnp.exp2((piece - now) * scale)
                    total[part, :] = acc
                    peak[part, :] = now
            return inner

        lax.fori_loop(0, n_one // 2, first_step, 0)

        @pl.when(after < n_z)
        def _():
            take_direct(dz_after)

        lax.fori_loop(n_one // 2, n_one, first_step, 0)

        for n, (peak, total, scale) in enumerate(((peak_s, sum_s, SCALE_S), (peak_t, sum_t, SCALE_T))):
            for g in range(tiles):
                part = slice(g * LANES, (g + 1) * LANES)
                lanes_peak = peak[part, :]
                top = jnp.max(lanes_peak, axis=1, keepdims=True)
                mass = jnp.sum(total[part, :] * jnp.exp2((lanes_peak - top) * scale), axis=1, keepdims=True)
                r = n * tiles + g
                lse_tile[r : r + 1, :] = to_row(top * scale + jnp.log(mass) * LOG2E)
        lse_send[z_at] = lse_tile[...]
        lse_all[z_at, me] = lse_tile[...]
        each(n_plane, lambda i: lse_copy(z_at, i).start())

        @pl.when(after < n_z)
        def _():
            take_handed(dz_after)

        return carry

    lax.fori_loop(0, n_z, chunk_step, 0)

    rows_across[...] = rows[:, :emb].T
    unit_acc[...] = jnp.zeros(unit_acc.shape, F32)

    each(n_plane, lambda i: push(
        ids.at[back(i)], ids.at[back(i)], id_ssem.at[i], id_rsem.at[back(i)], place(twin)
    ).wait_recv())
    lane = iota((1, LANES), 1)
    row_ratio = float(mask_count * PATCH_IMG // patch_count)
    for half in range(HALVES):
        id_rows = []
        for g in range(half * group_tiles, (half + 1) * group_tiles):
            id_rows.append(jnp.where(lane < mask_count, ids[2 * g], ids[2 * g + 1]))
        id_tile = jnp.concatenate(id_rows, axis=0)
        weight = jnp.zeros_like(id_tile)
        for label in range(IMG_GROUP):
            hits = jnp.where(id_tile == float(label), 1.0, 0.0)
            count = jnp.sum(jnp.sum(hits, axis=0, keepdims=True), axis=1, keepdims=True)
            weight = weight + hits * (row_ratio / jnp.maximum(count, 1.0))
        weight_tile[half * group_tiles : (half + 1) * group_tiles, :] = weight

    loss_acc[...] = jnp.zeros(loss_acc.shape, F32)
    for z_at in range(n_z):
        each(n_plane, lambda i: push(
            lse_send.at[z_at], lse_all.at[z_at, back(i)], lse_ssem.at[z_at, i], lse_rsem.at[z_at, back(i)], place(twin)
        ).wait_recv())
        top = lse_all[z_at, 0]
        for q in range(1, n_plane):
            top = jnp.maximum(top, lse_all[z_at, q])
        mass = jnp.exp2(lse_all[z_at, 0] - top)
        for q in range(1, n_plane):
            mass = mass + jnp.exp2(lse_all[z_at, q] - top)
        lse = top + jnp.log(mass) * LOG2E
        weight = weight_tile[z_at * tiles : (z_at + 1) * tiles, :]
        gain = jnp.log(weight / student_temp) * LOG2E
        lse_tile[:tiles, :] = lse[:tiles] - gain
        lse_tile[tiles:, :] = lse[tiles:] - gain
        loss_acc[:tiles, :] += weight * lse[:tiles] * LN2
        for g in range(tiles):
            part = slice(z_at * chunk + g * LANES, z_at * chunk + (g + 1) * LANES)
            shift_s[part, :] = jnp.broadcast_to(to_column(lse_tile[g : g + 1, :]), (LANES, LANES))
            shift_t[part, :] = jnp.broadcast_to(to_column(lse_tile[tiles + g : tiles + g + 1, :]), (LANES, LANES))

    cols_two = 512
    rows_two = 512
    n_two = cols // cols_two
    lag = 2
    loss_send[...] = jnp.zeros(loss_send.shape, F32)
    partner = (HALVES * y + 1 - zh, p)

    def block_at(j):
        return pl.ds(pl.multiple_of(j * cols_two, cols_two), cols_two)

    def slab_copy(j, i):
        to = lax.rem(y + i, n_y)
        return push(
            slab_send.at[to, :, block_at(j)],
            slab_recv.at[y, :, block_at(j)],
            slab_ssem.at[i, j],
            slab_rsem.at[y, j],
            y_peer(i),
        )

    def slab_arrival(j, i):
        origin = lax.rem(y + n_y - i, n_y)
        return push(
            slab_send.at[y, :, block_at(j)],
            slab_recv.at[origin, :, block_at(j)],
            slab_ssem.at[i, j],
            slab_rsem.at[origin, j],
            partner,
        )

    def half_copy(j):
        return push(half_send.at[:, block_at(j)], half_recv.at[:, block_at(j)], half_ssem.at[j], half_rsem.at[j], partner)

    def unit_copy(i_sem, q):
        return push(unit_send.at[span(q)], unit_recv.at[me], unit_ssem.at[i_sem], unit_rsem.at[me], place(q))

    def settle(j):
        block = block_at(j)
        for i in range(1, n_y):
            slab_arrival(j, i).wait_recv()
        acc = slab_send[y, :, block].astype(F32)
        for i in range(1, n_y):
            acc = acc + slab_recv[lax.rem(y + n_y - i, n_y), :, block].astype(F32)
        both[...] = acc.reshape(HALVES, part_rows, cols_two)
        proto_grad_out[:, pl.ds(pl.multiple_of(first_col + j * cols_two, cols_two), cols_two)] = both[zh]
        half_send[:, block] = both[1 - zh].astype(BF16)
        half_copy(j).start()

    def second_block(j, last):
        block = block_at(j)
        w_block = ws[:, block]
        wt_block = wt[:, block]
        shift = centre[:, pl.ds(pl.multiple_of(first_col + j * cols_two, cols_two), cols_two)] * SCALE_T
        acc = jnp.zeros((emb, cols_two), F32)
        cross = jnp.zeros((rows_two, LANES), F32)
        n_parts = n_rows // rows_two
        owners = rows_two // mask_count
        for r in range(n_parts):
            index = lax.rem(r + 1 + me // owners, n_parts) if last else r
            part = pl.ds(pl.multiple_of(index * rows_two, rows_two), rows_two)
            zs = jnp.dot(rows[part, :emb], w_block, preferred_element_type=F32)
            zt = jnp.dot(rows[part, emb:], wt_block, preferred_element_type=F32)
            a = shift_s[part, :]
            b = shift_t[part, :]
            pieces = []
            for n in range(cols_two // LANES):
                cut = slice(n * LANES, (n + 1) * LANES)
                logit = zs[:, cut]
                target = jnp.exp2(zt[:, cut] * SCALE_T - (b + shift[:, cut]))
                pieces.append((jnp.exp2(logit * SCALE_S - a) - target).astype(BF16))
                cross = cross + target * logit
            glog = jnp.concatenate(pieces, axis=1)
            product = lax.dot_general(glog, w_block, (((1,), (1,)), ((), ())), preferred_element_type=F32)
            acc = acc + jnp.dot(rows_across[:, part], glog, preferred_element_type=F32)
            if last:
                unit_send[part, :] = (unit_acc[part, :] + product).astype(BF16)
                for n in range(owners):
                    q = index * owners + n
                    if r < n_parts - 1:
                        unit_copy(r * owners + n, q).start()
                    else:

                        @pl.when(q != me)
                        def _():
                            unit_copy(r * owners + n, q).start()
            else:
                unit_acc[part, :] += product
        slab_send[:, :, block] = acc.astype(BF16).reshape(n_y, slab, cols_two)
        loss_send[...] += jnp.sum(jnp.sum(cross.reshape(rows_two // 8, 8, LANES), axis=0), axis=0, keepdims=True)
        for i in range(1, n_y):
            slab_copy(j, i).start()

    def second_step(j, carry):
        second_block(j, False)

        @pl.when(j >= lag)
        def _():
            settle(j - lag)

        return carry

    lax.fori_loop(0, n_two - 1, second_step, 0)
    second_block(n_two - 1, True)

    loss_recv[me] = loss_send[...]

    def loss_copy(i):
        return push(loss_send, loss_recv.at[me], loss_ssem.at[i], loss_rsem.at[me], place(ring(i)))

    each(n_plane, lambda i: loss_copy(i).start())
    unit_recv[me] = unit_send[span(me), :]
    settle(n_two - 1 - lag)
    settle(n_two - lag)

    each(n_plane, lambda i: push(
        loss_send, loss_recv.at[back(i)], loss_ssem.at[i], loss_rsem.at[back(i)], place(twin)
    ).wait_recv())
    cross_total = loss_recv[0]
    for q in range(1, n_plane):
        cross_total = cross_total + loss_recv[q]
    group_recv[y] = jnp.sum(loss_acc[...], axis=0, keepdims=True) - cross_total

    def group_copy(i):
        return push(group_recv.at[y], group_recv.at[y], group_ssem.at[i], group_rsem.at[y], y_peer(i))

    for i in range(1, n_y):
        group_copy(i).start()

    settle(n_two - 1)

    each(n_plane, lambda i: push(
        unit_send.at[span(me)], unit_recv.at[back(i)], unit_ssem.at[i], unit_rsem.at[back(i)], place(twin)
    ).wait_recv())
    unit_grad = unit_recv[0].astype(F32)
    for q in range(1, n_plane):
        unit_grad = unit_grad + unit_recv[q].astype(F32)
    raw = raw_keep[...]
    inv = inv_keep[:, 0:1]
    dotted = jnp.sum(raw * unit_grad, axis=1, keepdims=True)
    row_grad_out[...] = inv * unit_grad - (inv * inv * inv) * raw * dotted

    for i in range(1, n_y):
        q = lax.rem(y + n_y - i, n_y)
        push(group_recv.at[y], group_recv.at[q], group_ssem.at[i], group_rsem.at[q], partner).wait_recv()
    total = group_recv[0]
    for q in range(1, n_y):
        total = total + group_recv[q]
    loss_out[0, 0] = jnp.sum(total) * (1.0 / float(n_rows * n_y))

    other_col = (1 - zh) * cols
    for j in range(n_two):
        half_copy(j).wait_recv()
        to = pl.ds(pl.multiple_of(other_col + j * cols_two, cols_two), cols_two)
        proto_grad_out[:, to] = half_recv[:, j * cols_two : (j + 1) * cols_two].astype(F32)

    for dz in order:
        for dx in order:
            if dz or dx:
                row_copy(dz, dx).wait_send()
            hand_on(dz, dx).wait_send()

    def sent(i):
        id_copy(i).wait_send()
        loss_copy(i).wait_send()
        for z_at in range(n_z):
            lse_copy(z_at, i).wait_send()

    each(n_plane, sent)
    owners = rows_two // mask_count
    n_parts = n_rows // rows_two
    for r in range(n_parts):
        for n in range(owners):
            q = lax.rem(r + 1 + me // owners, n_parts) * owners + n
            if r < n_parts - 1:
                unit_copy(r * owners + n, q).wait_send()
            else:

                @pl.when(q != me)
                def _():
                    unit_copy(r * owners + n, q).wait_send()

    for j in range(n_two):
        half_copy(j).wait_send()
        for i in range(1, n_y):
            slab_copy(j, i).wait_send()
    for i in range(1, n_y):
        group_copy(i).wait_send()


def head(n_dp, n_proto, student_patch, teacher_patch, patch_image, masked_rows, student_proto, teacher_proto, centre):
    mask_count = masked_rows.shape[1]
    emb, all_cols = student_proto.shape
    cols = all_cols // HALVES
    n_plane = n_proto * HALVES
    n_y = n_dp // HALVES
    n_z = 2 * HALVES
    n_rows = mask_count * n_plane
    chunk = n_rows // n_z
    vmem = pl.BlockSpec(memory_space=pltpu.VMEM)
    hbm = pl.BlockSpec(memory_space=pl.ANY)
    dma = pltpu.SemaphoreType.DMA
    slab = emb // n_y
    blocks = cols // 512
    return pl.pallas_call(
        functools.partial(head_kernel, n_dp, n_proto),
        out_shape=(
            jax.ShapeDtypeStruct((mask_count, emb), F32),
            jax.ShapeDtypeStruct((slab // HALVES, all_cols), F32),
            jax.ShapeDtypeStruct((1, 1), F32),
        ),
        in_specs=[vmem, vmem, vmem, vmem, hbm, hbm, vmem],
        out_specs=(vmem, vmem, pl.BlockSpec(memory_space=pltpu.SMEM)),
        scratch_shapes=[
            pltpu.VMEM((4, emb, 1024), F32),
            pltpu.VMEM((emb, cols), BF16),
            pltpu.VMEM((emb, cols), BF16),
            pltpu.VMEM((n_rows, 2 * emb), BF16),
            pltpu.VMEM((emb, n_rows), BF16),
            pltpu.VMEM((mask_count, emb), F32),
            pltpu.VMEM((mask_count, LANES), F32),
            pltpu.VMEM((n_plane, 1, LANES), F32),
            pltpu.VMEM((chunk, LANES), F32),
            pltpu.VMEM((chunk, LANES), F32),
            pltpu.VMEM((chunk, LANES), F32),
            pltpu.VMEM((chunk, LANES), F32),
            pltpu.VMEM((n_rows, LANES), F32),
            pltpu.VMEM((n_rows, LANES), F32),
            pltpu.VMEM((n_rows // LANES, LANES), F32),
            pltpu.VMEM((8, LANES), F32),
            pltpu.VMEM((n_z, 8, LANES), F32),
            pltpu.VMEM((n_z, n_plane, 8, LANES), F32),
            pltpu.VMEM((n_rows, emb), F32),
            pltpu.VMEM((n_rows, emb), BF16),
            pltpu.VMEM((n_plane, mask_count, emb), BF16),
            pltpu.VMEM((n_y, slab, cols), BF16),
            pltpu.VMEM((n_y, slab, cols), BF16),
            pltpu.VMEM((HALVES, slab // HALVES, 512), F32),
            pltpu.VMEM((slab // HALVES, cols), BF16),
            pltpu.VMEM((slab // HALVES, cols), BF16),
            pltpu.VMEM((8, LANES), F32),
            pltpu.VMEM((1, LANES), F32),
            pltpu.VMEM((n_plane, 1, LANES), F32),
            pltpu.VMEM((n_y, 1, LANES), F32),
            dma((4,)),
            dma((n_plane // 2,)),
            dma((n_plane // 2,)),
            dma((n_plane,)),
            dma((n_plane,)),
            dma((n_plane,)),
            dma((n_z, n_plane)),
            dma((n_z, n_plane)),
            dma((n_plane,)),
            dma((n_plane,)),
            dma((n_y, blocks)),
            dma((n_y, blocks)),
            dma((blocks,)),
            dma((blocks,)),
            dma((n_plane,)),
            dma((n_plane,)),
            dma((n_y,)),
            dma((n_y,)),
        ],
        compiler_params=pltpu.CompilerParams(
            collective_id=0, has_side_effects=True, vmem_limit_bytes=56 * 1024 * 1024
        ),
        name="head",
    )(student_patch, teacher_patch, patch_image, masked_rows, student_proto, teacher_proto, centre)


def local(
    student_patch,
    teacher_patch,
    patch_image,
    masked_rows,
    student_proto,
    teacher_proto,
    first_moment,
    second_moment,
    centre,
):
    n_proto = lax.axis_size("proto")
    n_dp = lax.axis_size("dp")
    row_grad, proto_grad, loss = head(
        n_dp,
        n_proto,
        student_patch[0],
        teacher_patch[0],
        patch_image,
        masked_rows,
        student_proto,
        teacher_proto,
        centre[None, :],
    )
    slab_rows = first_moment.shape[0]
    slab_start = lax.axis_index("dp") * slab_rows
    own_student = lax.dynamic_slice_in_dim(student_proto, slab_start, slab_rows, 0)
    own_teacher = lax.dynamic_slice_in_dim(teacher_proto, slab_start, slab_rows, 0)
    new_first = beta_one * first_moment + (1.0 - beta_one) * proto_grad
    new_second = beta_two * second_moment + (1.0 - beta_two) * proto_grad * proto_grad
    step_size = new_first / fix_one / (jnp.sqrt(new_second / fix_two) + 1e-08)
    new_student = own_student - learn_rate * (step_size + decay_rate * own_student)
    new_teacher = teacher_keep * own_teacher + (1.0 - teacher_keep) * new_student
    return (row_grad[None], new_student, new_first, new_second, new_teacher, loss[0, 0])


def solution(mesh):
    in_specs = (
        P("dp", "proto", None),
        P("dp", "proto", None),
        P("dp", "proto"),
        P("dp", "proto"),
        P(None, "proto"),
        P(None, "proto"),
        P("dp", "proto"),
        P("dp", "proto"),
        P("proto"),
    )
    out_specs = (
        P("dp", "proto", None),
        P("dp", "proto"),
        P("dp", "proto"),
        P("dp", "proto"),
        P("dp", "proto"),
        P(),
    )
    return jax.shard_map(local, mesh=mesh, in_specs=in_specs, out_specs=out_specs, check_vma=False)
```

time: 116 us -> 104 us (0.90)
  Pallas kernels: 108 us -> 96.6 us
  between operations: 0.67 us -> 2.44 us
  local copies, waits for them, and re-layouts: 1.86 us -> 0.64 us
    pallas_call x1, Pallas kernels: 108 us -> 96.6 us  [head(): pl.pallas_call(functools.partial(head_kernel, n_dp, n_proto), out_shape=(...]
    slice x1 -> x0, local copies, waits for them, and re-layouts: 1.22 us -> none  [local(): loss[0, 0]]
where the time goes in v2:
time: 104 us
  Pallas kernels  96.6 us (93%)
  other arithmetic  4.47 us (4%)
  between operations  2.44 us (2%)
    pallas_call x1, Pallas kernels, head(): pl.pallas_call(functools.partial(head_kernel, n_dp, n_proto), out_shape=(...  96.6 us
    add x1, other arithmetic, local(): teacher_keep * own_teacher + (1.0 - teacher_keep) * new_student  4.47 us

profile of v2, /device:TPU:0, one launch (start us, length us, event | category | flops | bytes accessed | tf_op | source)
XLA Modules:
  0.0 104.2 jit_solution(13480958013487916185)
XLA Ops:
  0.6 0.0 copy-start
  0.6 0.0 copy-start.1
  0.7 96.6 %head.1 = (f32[64,256]{1,0:T(8,128)}, f32[32,8192]{1,0:T(8,128)}, f32[1,1]{1,0:T(1,128)}) custom-call(bf16[128,256]{1,0:T(8,128)(2,1)} %bitcast.5, bf16[128,256]{1,0:T(8,128)(2,1)} %bitcast.6, s32[1,128]{1,0:T(1,128)} %patch_image.1, s32[1,64]{1,0:T(1,128)} %masked_rows.1, f32[256,8192]{1,0:T(8,128)} %student_hbm.1, f32[256,8192]{1,0:T(8,128)} %teacher_hbm.1, ...), custom_call_target="tpu_custom_call" | custom-call | tf_op jit(solution)/shard_map/head/pallas_call | solution.py:582
  97.3 0.0 copy-start.2
  97.3 0.0 copy-done
  97.3 0.0 copy-done.1
  97.3 4.5 %multiply_add_fusion = (f32[32,8192]{1,0:T(8,128)}, f32[32,8192]{1,0:T(8,128)}, f32[32,8192]{1,0:T(8,128)}, f32[32,8192]{1,0:T(8,128)}) fusion(f32[256,8192]{1,0:T(8,128)} %teacher_hbm.1, s32[]{:T(128)S(6)} %select_n.4, f32[256,8192]{1,0:T(8,128)} %student_hbm.1, f32[32,8192]{1,0:T(8,128)} %get-tuple-element.10, f32[32,8192]{1,0:T(8,128)S(1)} %copy-done, ...), kind=kLoop, calls=%fused_computation.2 | loop fusion | flops 4718592 | bytes 9437188 | tf_op jit(solution)/shard_map/add | solution.py:680
  101.8 0.0 copy-done.2
  101.8 0.6 copy.17
Async XLA Ops:
  0.6 96.6 %copy-start = (f32[32,8192]{1,0:T(8,128)S(1)}, f32[32,8192]{1,0:T(8,128)}, u32[]{:S(2)}) copy-start(f32[32,8192]{1,0:T(8,128)} %param.15) | copy-start | bytes 3145732
  0.6 96.6 %copy-start.1 = (f32[32,8192]{1,0:T(8,128)S(1)}, f32[32,8192]{1,0:T(8,128)}, u32[]{:S(2)}) copy-start(f32[32,8192]{1,0:T(8,128)} %param.16) | copy-start | bytes 3145732
  97.3 4.5 %copy-start.2 = (f32[64,256]{1,0:T(8,128)S(1)}, f32[64,256]{1,0:T(8,128)}, u32[]{:S(2)}) copy-start(f32[64,256]{1,0:T(8,128)} %get-tuple-element.9) | copy-start | bytes 196612

commit v3 on v2

--- a/solution.py
+++ b/solution.py
@@ -54,16 +54,21 @@
 def head_kernel(
     n_dp,
     n_proto,
+    student_patch_hbm,
+    teacher_patch_hbm,
+    patch_image_hbm,
+    masked_rows_hbm,
+    student_hbm,
+    teacher_hbm,
+    centre_hbm,
+    row_grad_out,
+    proto_grad_out,
+    loss_out,
     student_patch,
     teacher_patch,
     patch_image,
     masked_rows,
-    student_hbm,
-    teacher_hbm,
     centre,
-    row_grad_out,
-    proto_grad_out,
-    loss_out,
     stage,
     ws,
     wt,
@@ -85,6 +90,7 @@
     unit_acc,
     unit_send,
     unit_recv,
+    twin_recv,
     slab_send,
     slab_recv,
     both,
@@ -94,6 +100,7 @@
     loss_send,
     loss_recv,
     group_recv,
+    input_sem,
     stage_sem,
     row_ssem,
     hand_ssem,
@@ -104,6 +111,8 @@
     lse_rsem,
     unit_ssem,
     unit_rsem,
+    twin_ssem,
+    twin_rsem,
     slab_ssem,
     slab_rsem,
     half_ssem,
@@ -160,6 +169,19 @@
 
         lax.fori_loop(1, count, step, 0)
 
+    inputs = []
+    for n, (src, dst) in enumerate(
+        (
+            (masked_rows_hbm, masked_rows),
+            (student_patch_hbm, student_patch),
+            (teacher_patch_hbm, teacher_patch),
+            (patch_image_hbm, patch_image),
+            (centre_hbm, centre),
+        )
+    ):
+        inputs.append(pltpu.make_async_copy(src, dst, input_sem.at[n]))
+        inputs[-1].start()
+
     barrier = pltpu.get_barrier_semaphore()
 
     def y_peer(i):
@@ -179,6 +201,8 @@
     load(student_hbm, 1, 2).start()
     load(teacher_hbm, 1, 3).start()
 
+    for copy in inputs:
+        copy.wait()
     picked = to_column(masked_rows[...].astype(F32))
     one_hot = iota((mask_count, patch_count), 1).astype(F32) == picked
     one_hot_f = jnp.where(one_hot, 1.0, 0.0)
@@ -409,8 +433,32 @@
     def half_copy(j):
         return push(half_send.at[:, block_at(j)], half_recv.at[:, block_at(j)], half_ssem.at[j], half_rsem.at[j], partner)
 
-    def unit_copy(i_sem, q):
-        return push(unit_send.at[span(q)], unit_recv.at[me], unit_ssem.at[i_sem], unit_rsem.at[me], place(q))
+    n_chips = n_plane // 2
+
+    def twin_copy(chip):
+        block = span(2 * chip + 1 - core)
+        return push(unit_send.at[block], twin_recv.at[chip], twin_ssem.at[chip], twin_rsem.at[chip], place(twin))
+
+    def unit_copy(chip):
+        q = 2 * chip + core
+        return push(
+            unit_send.at[span(q)], unit_recv.at[me // 2], unit_ssem.at[chip], unit_rsem.at[me // 2], place(q)
+        )
+
+    def merge(index, chips, own_plane):
+        for n in range(chips):
+            chip = index * chips + n
+            twin_copy(chip).wait_recv()
+            block = span(2 * chip + core)
+            both_terms = unit_send[block, :].astype(F32) + twin_recv[chip].astype(F32)
+            unit_send[block, :] = both_terms.astype(BF16)
+            if own_plane:
+
+                @pl.when(chip != me // 2)
+                def _():
+                    unit_copy(chip).start()
+            else:
+                unit_copy(chip).start()
 
     def settle(j):
         block = block_at(j)
@@ -452,15 +500,10 @@
             acc = acc + jnp.dot(rows_across[:, part], glog, preferred_element_type=F32)
             if last:
                 unit_send[part, :] = (unit_acc[part, :] + product).astype(BF16)
-                for n in range(owners):
-                    q = index * owners + n
-                    if r < n_parts - 1:
-                        unit_copy(r * owners + n, q).start()
-                    else:
-
-                        @pl.when(q != me)
-                        def _():
-                            unit_copy(r * owners + n, q).start()
+                for n in range(owners // 2):
+                    twin_copy(index * (owners // 2) + n).start()
+                if r > 0:
+                    merge(lax.rem(r + me // owners, n_parts), owners // 2, False)
             else:
                 unit_acc[part, :] += product
         slab_send[:, :, block] = acc.astype(BF16).reshape(n_y, slab, cols_two)
@@ -480,13 +523,16 @@
     lax.fori_loop(0, n_two - 1, second_step, 0)
     second_block(n_two - 1, True)
 
+    plane_devices = rows_two // mask_count
+    merge(me // plane_devices, plane_devices // 2, True)
+    unit_recv[me // 2] = unit_send[span(me), :]
+
     loss_recv[me] = loss_send[...]
 
     def loss_copy(i):
         return push(loss_send, loss_recv.at[me], loss_ssem.at[i], loss_rsem.at[me], place(ring(i)))
 
     each(n_plane, lambda i: loss_copy(i).start())
-    unit_recv[me] = unit_send[span(me), :]
     settle(n_two - 1 - lag)
     settle(n_two - lag)
 
@@ -506,12 +552,16 @@
 
     settle(n_two - 1)
 
-    each(n_plane, lambda i: push(
-        unit_send.at[span(me)], unit_recv.at[back(i)], unit_ssem.at[i], unit_rsem.at[back(i)], place(twin)
-    ).wait_recv())
+    def unit_take(i):
+        chip = lax.rem(me // 2 + n_chips - i, n_chips)
+        push(
+            unit_send.at[span(me)], unit_recv.at[chip], unit_ssem.at[i], unit_rsem.at[chip], place(twin)
+        ).wait_recv()
+
+    each(n_chips, unit_take)
     unit_grad = unit_recv[0].astype(F32)
-    for q in range(1, n_plane):
-        unit_grad = unit_grad + unit_recv[q].astype(F32)
+    for chip in range(1, n_chips):
+        unit_grad = unit_grad + unit_recv[chip].astype(F32)
     raw = raw_keep[...]
     inv = inv_keep[:, 0:1]
     dotted = jnp.sum(raw * unit_grad, axis=1, keepdims=True)
@@ -544,18 +594,12 @@
             lse_copy(z_at, i).wait_send()
 
     each(n_plane, sent)
-    owners = rows_two // mask_count
-    n_parts = n_rows // rows_two
-    for r in range(n_parts):
-        for n in range(owners):
-            q = lax.rem(r + 1 + me // owners, n_parts) * owners + n
-            if r < n_parts - 1:
-                unit_copy(r * owners + n, q).wait_send()
-            else:
-
-                @pl.when(q != me)
-                def _():
-                    unit_copy(r * owners + n, q).wait_send()
+    for chip in range(n_chips):
+        twin_copy(chip).wait_send()
+
+        @pl.when(chip != me // 2)
+        def _():
+            unit_copy(chip).wait_send()
 
     for j in range(n_two):
         half_copy(j).wait_send()
@@ -586,9 +630,14 @@
             jax.ShapeDtypeStruct((slab // HALVES, all_cols), F32),
             jax.ShapeDtypeStruct((1, 1), F32),
         ),
-        in_specs=[vmem, vmem, vmem, vmem, hbm, hbm, vmem],
+        in_specs=[hbm] * 7,
         out_specs=(vmem, vmem, pl.BlockSpec(memory_space=pltpu.SMEM)),
         scratch_shapes=[
+            pltpu.VMEM(student_patch.shape, BF16),
+            pltpu.VMEM(teacher_patch.shape, BF16),
+            pltpu.VMEM(patch_image.shape, jnp.int32),
+            pltpu.VMEM(masked_rows.shape, jnp.int32),
+            pltpu.VMEM(centre.shape, F32),
             pltpu.VMEM((4, emb, 1024), F32),
             pltpu.VMEM((emb, cols), BF16),
             pltpu.VMEM((emb, cols), BF16),
@@ -609,7 +658,8 @@
             pltpu.VMEM((n_z, n_plane, 8, LANES), F32),
             pltpu.VMEM((n_rows, emb), F32),
             pltpu.VMEM((n_rows, emb), BF16),
-            pltpu.VMEM((n_plane, mask_count, emb), BF16),
+            pltpu.VMEM((n_plane // 2, mask_count, emb), BF16),
+            pltpu.VMEM((n_plane // 2, mask_count, emb), BF16),
             pltpu.VMEM((n_y, slab, cols), BF16),
             pltpu.VMEM((n_y, slab, cols), BF16),
             pltpu.VMEM((HALVES, slab // HALVES, 512), F32),
@@ -619,6 +669,7 @@
             pltpu.VMEM((1, LANES), F32),
             pltpu.VMEM((n_plane, 1, LANES), F32),
             pltpu.VMEM((n_y, 1, LANES), F32),
+            dma((5,)),
             dma((4,)),
             dma((n_plane // 2,)),
             dma((n_plane // 2,)),
@@ -627,8 +678,10 @@
             dma((n_plane,)),
             dma((n_z, n_plane)),
             dma((n_z, n_plane)),
-            dma((n_plane,)),
-            dma((n_plane,)),
+            dma((n_plane // 2,)),
+            dma((n_plane // 2,)),
+            dma((n_plane // 2,)),
+            dma((n_plane // 2,)),
             dma((n_y, blocks)),
             dma((n_y, blocks)),
             dma((blocks,)),

time: 104 us -> 98.6 us (0.948)
  Pallas kernels: 96.6 us -> 90.9 us
    pallas_call x1, Pallas kernels: 96.6 us -> 90.9 us  [head(): pl.pallas_call(functools.partial(head_kernel, n_dp, n_proto), out_shape=(...]
where the time goes in v3:
time: 98.6 us; the launch traced here: 98.5 us
  Pallas kernels  90.9 us (92%)
  other arithmetic  4.47 us (5%)
  between operations  2.44 us (2%)
    pallas_call x1, Pallas kernels, head(): pl.pallas_call(functools.partial(head_kernel, n_dp, n_proto), out_shape=(...  90.9 us
    add x1, other arithmetic, local(): teacher_keep * own_teacher + (1.0 - teacher_keep) * new_student  4.47 us

profile of v3, /device:TPU:0, one launch (start us, length us, event | category | flops | bytes accessed | tf_op | source)
XLA Modules:
  0.0 98.5 jit_solution(2589692639499850167)
XLA Ops:
  0.6 0.0 copy-start
  0.6 0.0 copy-start.1
  0.7 90.9 %head.1 = (f32[64,256]{1,0:T(8,128)}, f32[32,8192]{1,0:T(8,128)}, f32[1,1]{1,0:T(1,128)}) custom-call(bf16[128,256]{1,0:T(8,128)(2,1)} %bitcast.5, bf16[128,256]{1,0:T(8,128)(2,1)} %bitcast.6, s32[1,128]{1,0:T(1,128)} %patch_image_hbm.1, s32[1,64]{1,0:T(1,128)} %masked_rows_hbm.1, f32[256,8192]{1,0:T(8,128)} %student_hbm.1, f32[256,8192]{1,0:T(8,128)} %teacher_hbm.1, ...), custom_call_target="tpu_custom_call" | custom-call | tf_op jit(solution)/shard_map/head/pallas_call | solution.py:626
  91.6 0.0 copy-start.2
  91.6 0.0 copy-done
  91.6 0.0 copy-done.1
  91.6 4.5 %multiply_add_fusion = (f32[32,8192]{1,0:T(8,128)}, f32[32,8192]{1,0:T(8,128)}, f32[32,8192]{1,0:T(8,128)}, f32[32,8192]{1,0:T(8,128)}) fusion(f32[256,8192]{1,0:T(8,128)} %teacher_hbm.1, s32[]{:T(128)S(6)} %select_n.4, f32[256,8192]{1,0:T(8,128)} %student_hbm.1, f32[32,8192]{1,0:T(8,128)} %get-tuple-element.10, f32[32,8192]{1,0:T(8,128)S(1)} %copy-done, ...), kind=kLoop, calls=%fused_computation.2 | loop fusion | flops 4718592 | bytes 9437188 | tf_op jit(solution)/shard_map/add | solution.py:733
  96.1 0.0 copy-done.2
  96.1 0.6 copy.17
Async XLA Ops:
  0.6 91.0 %copy-start = (f32[32,8192]{1,0:T(8,128)S(1)}, f32[32,8192]{1,0:T(8,128)}, u32[]{:S(2)}) copy-start(f32[32,8192]{1,0:T(8,128)} %param.15) | copy-start | bytes 3145732
  0.6 91.0 %copy-start.1 = (f32[32,8192]{1,0:T(8,128)S(1)}, f32[32,8192]{1,0:T(8,128)}, u32[]{:S(2)}) copy-start(f32[32,8192]{1,0:T(8,128)} %param.16) | copy-start | bytes 3145732
  91.6 4.5 %copy-start.2 = (f32[64,256]{1,0:T(8,128)S(1)}, f32[64,256]{1,0:T(8,128)}, u32[]{:S(2)}) copy-start(f32[64,256]{1,0:T(8,128)} %get-tuple-element.9) | copy-start | bytes 196612

commit v4 on v3

--- a/solution.py
+++ b/solution.py
@@ -30,6 +30,8 @@
 SCALE_T = LOG2E / teacher_temp
 LOWEST = -3.0e38
 LANES = 128
+SMALLEST = 1.0e-25
+LARGEST = 1.0e30
 HALVES = 2
 
 
@@ -52,6 +54,7 @@
 
 
 def head_kernel(
+    guarded,
     n_dp,
     n_proto,
     student_patch_hbm,
@@ -287,7 +290,7 @@
     take_direct(0, skip_own=True)
     take_handed(0)
 
-    cols_one = 512
+    cols_one = 512 if guarded else 2048
     n_one = cols // cols_one
 
     def lse_copy(k_at, i):
@@ -316,6 +319,16 @@
                     logit = jnp.dot(
                         rows[here, e0 : e0 + emb], w[:, pl.ds(c0, cols_one)], preferred_element_type=F32
                     )
+                    if not guarded:
+                        acc = total[part, :]
+                        for n in range(cols_one // LANES):
+                            power = logit[:, n * LANES : (n + 1) * LANES] * scale
+                            if shift:
+                                at_col = pl.multiple_of(first_col + c0 + n * LANES, LANES)
+                                power = power - centre[:, pl.ds(at_col, LANES)] * scale
+                            acc = acc + jnp.exp2(power)
+                        total[part, :] = acc
+                        continue
                     if shift:
                         logit = logit - centre[:, pl.ds(pl.multiple_of(first_col + c0, cols_one), cols_one)]
                     pieces = [logit[:, n * LANES : (n + 1) * LANES] for n in range(cols_one // LANES)]
@@ -341,6 +354,12 @@
         for n, (peak, total, scale) in enumerate(((peak_s, sum_s, SCALE_S), (peak_t, sum_t, SCALE_T))):
             for g in range(tiles):
                 part = slice(g * LANES, (g + 1) * LANES)
+                if not guarded:
+                    mass = jnp.sum(total[part, :], axis=1, keepdims=True)
+                    usable = jnp.logical_and(mass > SMALLEST, mass < LARGEST)
+                    r = n * tiles + g
+                    lse_tile[r : r + 1, :] = to_row(jnp.where(usable, jnp.log(mass) * LOG2E, jnp.nan))
+                    continue
                 lanes_peak = peak[part, :]
                 top = jnp.max(lanes_peak, axis=1, keepdims=True)
                 mass = jnp.sum(total[part, :] * jnp.exp2((lanes_peak - top) * scale), axis=1, keepdims=True)
@@ -609,7 +628,7 @@
         group_copy(i).wait_send()
 
 
-def head(n_dp, n_proto, student_patch, teacher_patch, patch_image, masked_rows, student_proto, teacher_proto, centre):
+def head(guarded, n_dp, n_proto, student_patch, teacher_patch, patch_image, masked_rows, student_proto, teacher_proto, centre):
     mask_count = masked_rows.shape[1]
     emb, all_cols = student_proto.shape
     cols = all_cols // HALVES
@@ -624,7 +643,7 @@
     slab = emb // n_y
     blocks = cols // 512
     return pl.pallas_call(
-        functools.partial(head_kernel, n_dp, n_proto),
+        functools.partial(head_kernel, guarded, n_dp, n_proto),
         out_shape=(
             jax.ShapeDtypeStruct((mask_count, emb), F32),
             jax.ShapeDtypeStruct((slab // HALVES, all_cols), F32),
@@ -692,9 +711,9 @@
             dma((n_y,)),
         ],
         compiler_params=pltpu.CompilerParams(
-            collective_id=0, has_side_effects=True, vmem_limit_bytes=56 * 1024 * 1024
+            collective_id=int(guarded), has_side_effects=True, vmem_limit_bytes=56 * 1024 * 1024
         ),
-        name="head",
+        name="head_guarded" if guarded else "head",
     )(student_patch, teacher_patch, patch_image, masked_rows, student_proto, teacher_proto, centre)
 
 
@@ -711,9 +730,7 @@
 ):
     n_proto = lax.axis_size("proto")
     n_dp = lax.axis_size("dp")
-    row_grad, proto_grad, loss = head(
-        n_dp,
-        n_proto,
+    operands = (
         student_patch[0],
         teacher_patch[0],
         patch_image,
@@ -721,6 +738,10 @@
         student_proto,
         teacher_proto,
         centre[None, :],
+    )
+    quick = head(False, n_dp, n_proto, *operands)
+    row_grad, proto_grad, loss = lax.cond(
+        jnp.isnan(quick[2][0, 0]), lambda: head(True, n_dp, n_proto, *operands), lambda: quick
     )
     slab_rows = first_moment.shape[0]
     slab_start = lax.axis_index("dp") * slab_rows

time: 98.6 us -> 175 us (1.77)
  Pallas kernels: 90.9 us -> 166 us
    pallas_call x1 -> x2, Pallas kernels: 90.9 us -> 166 us  [head(): pl.pallas_call(functools.partial(head_kernel, guarded, n_dp, n_proto), ou...]
where the time goes in v4:
time: 175 us
  Pallas kernels  166 us (95%)
  other arithmetic  4.15 us (2%)
  between operations  3.8 us (2%)
    pallas_call x2, Pallas kernels, head(): pl.pallas_call(functools.partial(head_kernel, guarded, n_dp, n_proto), ou...  166 us
    add x1, other arithmetic, local(): teacher_keep * own_teacher + (1.0 - teacher_keep) * new_student  4.15 us

profile of v4, /device:TPU:0, one launch (start us, length us, event | category | flops | bytes accessed | tf_op | source)
XLA Modules:
  0.0 175.0 jit_solution(9523402566738704361)
XLA Ops:
  0.6 0.0 copy-start.2
  0.6 0.0 copy-start.3
  0.7 0.0 copy-start.4
  0.7 0.0 copy-start.5
  0.7 0.0 copy-start.6
  0.7 80.0 %head.1 = (f32[64,256]{1,0:T(8,128)S(1)}, f32[32,8192]{1,0:T(8,128)S(1)}, f32[1,1]{1,0:T(1,128)}) custom-call(bf16[128,256]{1,0:T(8,128)(2,1)} %bitcast.6, bf16[128,256]{1,0:T(8,128)(2,1)} %bitcast.8, s32[1,128]{1,0:T(1,128)} %patch_image_hbm.1, s32[1,64]{1,0:T(1,128)} %masked_rows_hbm.1, f32[256,8192]{1,0:T(8,128)} %student_hbm.1, f32[256,8192]{1,0:T(8,128)} %teacher_hbm.1, ...), custom_call_target="tpu_custom_call" | custom-call | tf_op jit(solution)/shard_map/head/pallas_call | solution.py:645
  82.0 0.0 copy-done.2
  82.0 0.0 copy-done.3
  82.0 0.0 copy-done.4
  82.0 0.0 copy-done.5
  82.0 0.0 copy-done.6
  82.0 0.0 copy-start
  82.0 0.0 copy-start.1
  82.1 86.4 %conditional.1 = ((f32[32,8192]{1,0:T(8,128)S(1)}, f32[64,256]{1,0:T(8,128)S(1)}, f32[1,1]{1,0:T(1,128)})) conditional(s32[]{:T(128)} %bitcast.3, (f32[32,8192]{1,0:T(8,128)S(1)}, f32[64,256]{1,0:T(8,128)S(1)}, f32[1,1]{1,0:T(1,128)}) %tuple.22, (bf16[128,256]{1,0:T(8,128)(2,1)S(1)}, bf16[128,256]{1,0:T(8,128)(2,1)S(1)}, s32[1,128]{1,0:T(1,128)S(1)}, ...), branch_computations={%region_0.0_spmd, %region_1.0_spmd} | conditional | bytes 32 | solution.py:743
  82.1 86.2 %head_guarded.1 = (f32[64,256]{1,0:T(8,128)S(1)}, f32[32,8192]{1,0:T(8,128)S(1)}, f32[1,1]{1,0:T(1,128)}) custom-call(bf16[128,256]{1,0:T(8,128)(2,1)S(1)} %get-tuple-element.31.student_patch_hbm, bf16[128,256]{1,0:T(8,128)(2,1)S(1)} %get-tuple-element.32.teacher_patch_hbm, s32[1,128]{1,0:T(1,128)S(1)} %get-tuple-element.33.patch_image_hbm, ...), custom_call_target="tpu_custom_call" | custom-call | tf_op jit(solution)/shard_map/cond/branch_1_fun/head_guarded/pallas_call | solution.py:645
  168.5 0.0 copy-done
  168.5 0.0 copy-done.1
  168.5 4.2 %multiply_add_fusion = (f32[32,8192]{1,0:T(8,128)}, f32[32,8192]{1,0:T(8,128)}, f32[32,8192]{1,0:T(8,128)}, f32[32,8192]{1,0:T(8,128)}) fusion(f32[256,8192]{1,0:T(8,128)} %teacher_hbm.1, s32[]{:T(128)S(6)} %select_n.4, f32[256,8192]{1,0:T(8,128)} %student_hbm.1, f32[32,8192]{1,0:T(8,128)S(1)} %get-tuple-element.64, f32[32,8192]{1,0:T(8,128)S(1)} %copy-done, ...), kind=kLoop, calls=%fused_computation.2 | loop fusion | flops 4718592 | bytes 9437188 | tf_op jit(solution)/shard_map/add | solution.py:754
  172.6 0.6 copy.23
Async XLA Ops:
  0.6 81.3 %copy-start.2 = (bf16[1,128,256]{2,1,0:T(8,128)(2,1)S(1)}, bf16[1,128,256]{2,1,0:T(8,128)(2,1)}, u32[]{:S(2)}) copy-start(bf16[1,128,256]{2,1,0:T(8,128)(2,1)} %param.11) | copy-start | bytes 196612
  0.6 81.3 %copy-start.3 = (bf16[1,128,256]{2,1,0:T(8,128)(2,1)S(1)}, bf16[1,128,256]{2,1,0:T(8,128)(2,1)}, u32[]{:S(2)}) copy-start(bf16[1,128,256]{2,1,0:T(8,128)(2,1)} %param.12) | copy-start | bytes 196612
  0.7 81.3 %copy-start.4 = (f32[8192]{0:T(1024)S(1)}, f32[8192]{0:T(1024)}, u32[]{:S(2)}) copy-start(f32[8192]{0:T(1024)} %param.19) | copy-start | bytes 98308
  0.7 81.3 %copy-start.5 = (s32[1,128]{1,0:T(1,128)S(1)}, s32[1,128]{1,0:T(1,128)}, u32[]{:S(2)}) copy-start(s32[1,128]{1,0:T(1,128)} %patch_image_hbm.1) | copy-start | bytes 1540
  0.7 81.3 %copy-start.6 = (s32[1,64]{1,0:T(1,128)S(1)}, s32[1,64]{1,0:T(1,128)}, u32[]{:S(2)}) copy-start(s32[1,64]{1,0:T(1,128)} %masked_rows_hbm.1) | copy-start | bytes 772
  82.0 86.4 %copy-start = (f32[32,8192]{1,0:T(8,128)S(1)}, f32[32,8192]{1,0:T(8,128)}, u32[]{:S(2)}) copy-start(f32[32,8192]{1,0:T(8,128)} %param.17) | copy-start | bytes 3145732
  82.0 86.4 %copy-start.1 = (f32[32,8192]{1,0:T(8,128)S(1)}, f32[32,8192]{1,0:T(8,128)}, u32[]{:S(2)}) copy-start(f32[32,8192]{1,0:T(8,128)} %param.18) | copy-start | bytes 3145732
